TPU v7x, 128 devices: a whole 4x4x4 slice. The times are simulated.
128 devices in a mesh: node: 4 (over z_hi, core), wide: 32 (over z_lo, y, x).
Axes of the slice: x: 4, y: 4, z: 4 (z_hi: 2, z_lo: 2; z = z_hi * 2 + z_lo), core: 2. Of those that a mesh axis runs over, the one named last changes fastest.
Arguments:
- tokens: bfloat16 [8192, 4096], P(('node', 'wide')), may hold values from -6 to 6
- expert_ids: int32 [8192, 6], P(('node', 'wide')), may hold values from 0 to 127, all different within a row; in each aligned block of 64 rows (0 to 63, 64 to 127, ...) at most 4 rows name the same one
- gate_weights: float32 [8192, 6], P(('node', 'wide')), may hold values from 0.1 to 1
- w_gate: bfloat16 [128, 4096, 768], P(('node', 'wide')), may hold values from -0.09375 to 0.09375
- w_up: bfloat16 [128, 4096, 768], P(('node', 'wide')), may hold values from -0.09375 to 0.09375
- w_down: bfloat16 [128, 768, 4096], P(('node', 'wide')), may hold values from -0.21875 to 0.21875
- gate_scale: float32 [128, 768], P(('node', 'wide')), may hold values from 0.5 to 2
- up_scale: float32 [128, 768], P(('node', 'wide')), may hold values from 0.5 to 2
- down_scale: float32 [128, 4096], P(('node', 'wide')), may hold values from 0.5 to 2
Outputs:
- mixed: bfloat16 [8192, 4096], P(('node', 'wide'))
Inputs may be any that keep to these rules, and one draw needn't show every extreme that they name: `expert_ids`: each token names 6 different experts; among the routes of the tokens of one device no expert is named more than 4 times, a bound that some block reaches.
All inputs are finite; a program needn't handle non-finite values.
Results may differ from a plain program's by a relative error of at most 0.0058.
Values may be sent and summed in bfloat16 or wider, within the bound.
No kernel may reach another device: no remote copies, remote signals or barrier semaphores. Data moves between devices by JAX's collectives and lax.ppermute only.
A program may use at most 128 MiB of HBM per device.

v0:
```python
import jax
import jax.numpy as jnp
from jax import lax
from jax.sharding import PartitionSpec as P


def expert_block(received, w_gate, w_up, w_down, gate_scale, up_scale, down_scale):
    shape = received.shape
    rows = received.reshape(-1, shape[-1])
    gate = jnp.dot(rows, w_gate[0], preferred_element_type=jnp.float32) * gate_scale[0]
    up = jnp.dot(rows, w_up[0], preferred_element_type=jnp.float32) * up_scale[0]
    hidden = (jax.nn.silu(gate) * up).astype(jnp.bfloat16)
    routed = jnp.dot(hidden, w_down[0], preferred_element_type=jnp.float32) * down_scale[0]
    return routed.astype(jnp.bfloat16).reshape(shape)


def on_device(
    tokens, expert_ids, gate_weights, w_gate, w_up, w_down, gate_scale, up_scale, down_scale
):
    count, top = expert_ids.shape
    width = tokens.shape[1]
    experts = lax.axis_size(("node", "wide"))
    capacity = max(2, 4 * count * top // (3 * experts))
    flat_ids = expert_ids.reshape(-1)
    picked = (flat_ids[:, None] == jnp.arange(experts, dtype=jnp.int32)[None, :]).astype(jnp.int32)
    before = jnp.cumsum(picked, axis=0) - picked
    position = jnp.sum(before * picked, axis=1)
    slots = flat_ids * capacity + position
    place = slots[:, None] == jnp.arange(experts * capacity, dtype=jnp.int32)[None, :]
    dispatch = jnp.sum(
        place.reshape(count, top, experts * capacity).astype(jnp.float32), axis=1
    ).astype(jnp.bfloat16)
    packed = lax.dot_general(
        dispatch, tokens, (((0,), (0,)), ((), ())), preferred_element_type=jnp.float32
    )
    packed = packed.astype(jnp.bfloat16).reshape(experts, capacity, width)
    returned = lax.all_to_all(
        expert_block(
            lax.all_to_all(packed, ("node", "wide"), split_axis=0, concat_axis=0, tiled=True),
            w_gate,
            w_up,
            w_down,
            gate_scale,
            up_scale,
            down_scale,
        ),
        ("node", "wide"),
        split_axis=0,
        concat_axis=0,
        tiled=True,
    )
    results = returned.reshape(experts * capacity, width)
    chosen = results[slots].reshape(count, top, width).astype(jnp.float32)
    mixed = jnp.sum(chosen * gate_weights[:, :, None], axis=1)
    return mixed.astype(jnp.bfloat16)


def solution(mesh):
    placed = (
        P(("node", "wide"), None),
        P(("node", "wide"), None),
        P(("node", "wide"), None),
        P(("node", "wide"), None, None),
        P(("node", "wide"), None, None),
        P(("node", "wide"), None, None),
        P(("node", "wide"), None),
        P(("node", "wide"), None),
        P(("node", "wide"), None),
    )
    return jax.shard_map(
        on_device, mesh=mesh, in_specs=placed, out_specs=P(("node", "wide"), None), check_vma=False
    )
```

profile of v0, /device:TPU:1, one launch (start us, length us, event | category | flops | bytes accessed | tf_op | source)
XLA Modules:
  0.0 201.8 jit_solution(7004146398543736934)
XLA Ops:
  0.0 0.0 copy-start
  0.0 0.8 copy.18
  0.8 0.1 eq.43
  1.0 0.1 eq.39
  1.1 0.1 copy.21
  1.2 0.2 fusion.9
  1.5 0.1 broadcast_add_fusion
  1.6 0.2 fusion.12
  1.8 0.1 reduce_sum.32
  2.0 0.1 copy.23
  2.0 0.2 convert_reduce_fusion
  2.2 0.0 copy-done
  2.2 3.2 %convolution_convert_fusion = bf16[512,4096]{1,0:T(8,128)(2,1)} fusion(bf16[64,4096]{1,0:T(8,128)(2,1)S(1)} %copy-done, bf16[64,512]{1,0:T(8,128)(2,1)S(1)} %convert_reduce_fusion), kind=kOutput, calls=%fused_computation.8 | convolution fusion | flops 270532608 | bytes 4784128 | tf_op jit(solution)/shard_map/dot_general | solution.py:33
  5.4 7.2 %reshape.77 = bf16[128,4,4096]{2,1,0:T(4,128)(2,1)} reshape(bf16[512,4096]{1,0:T(8,128)(2,1)} %convolution_convert_fusion) | data formatting | bytes 8388608 | tf_op jit(solution)/shard_map/reshape | solution.py:36
  12.6 11.9 %all-to-all-start = ((bf16[128,4,4096]{2,1,0:T(4,128)(2,1)}), bf16[128,4,4096]{2,1,0:T(4,128)(2,1)}, u32[]{:S(2)}, u32[]{:S(2)}) async-start(bf16[128,4,4096]{2,1,0:T(4,128)(2,1)} %reshape.77), calls=%async_computation | async-start | bytes 8388608 | tf_op jit(solution)/shard_map/all_to_all | solution.py:39
  24.6 0.0 copy-done.3
  24.6 0.0 copy-done.4
  24.6 51.1 %all-to-all-done = bf16[128,4,4096]{2,1,0:T(4,128)(2,1)} async-done(((bf16[128,4,4096]{2,1,0:T(4,128)(2,1)}), bf16[128,4,4096]{2,1,0:T(4,128)(2,1)}, u32[]{:S(2)}, u32[]{:S(2)}) %all-to-all-start) | async-done | bytes 4194336 | tf_op jit(solution)/shard_map/all_to_all | solution.py:39
  75.7 6.9 %reshape.78 = bf16[512,4096]{1,0:T(8,128)(2,1)} reshape(bf16[128,4,4096]{2,1,0:T(4,128)(2,1)} %all-to-all-done) | data formatting | bytes 8388608 | tf_op jit(solution)/shard_map/reshape | solution.py:9
  82.6 7.0 %fusion.1 = f32[512,768]{1,0:T(8,128)S(1)} fusion(bf16[512,4096]{1,0:T(8,128)(2,1)} %reshape.78, bf16[1,4096,768]{2,1,0:T(8,128)(2,1)} %param.13), kind=kOutput, calls=%fused_computation.4 | convolution fusion | flops 3221225472 | bytes 12058624 | tf_op jit(solution)/shard_map/dot_general | solution.py:11
  89.7 0.0 copy-done.5
  89.7 16.6 %multiply_convert_fusion = bf16[512,4096]{1,0:T(8,128)(2,1)} fusion(bf16[1,768,4096]{2,1,0:T(8,128)(2,1)} %param.14, f32[4096]{0:T(1024)S(1)} %bitcast.30, f32[512,768]{1,0:T(8,128)S(1)} %fusion.1, bf16[512,4096]{1,0:T(8,128)(2,1)} %reshape.78, bf16[1,4096,768]{2,1,0:T(8,128)(2,1)} %param.12, f32[768]{0:T(1024)S(1)} %reduce.1, f32[768]{0:T(1024)S(1)} %reduce), kind=kOutput, calls=%fused_computation.2 | convolution fusion | flops 6449790976 | bytes 22566912 | tf_op jit(solution)/shard_map/dot_general | solution.py:13
  106.3 7.2 %reshape.79 = bf16[128,4,4096]{2,1,0:T(4,128)(2,1)} reshape(bf16[512,4096]{1,0:T(8,128)(2,1)} %multiply_convert_fusion) | data formatting | bytes 8388608 | tf_op jit(solution)/shard_map/reshape | solution.py:14
  113.5 5.8 %all-to-all-start.1 = ((bf16[128,4,4096]{2,1,0:T(4,128)(2,1)}), bf16[128,4,4096]{2,1,0:T(4,128)(2,1)}, u32[]{:S(2)}, u32[]{:S(2)}) async-start(bf16[128,4,4096]{2,1,0:T(4,128)(2,1)} %reshape.79), calls=%async_computation.1 | async-start | bytes 8388608 | tf_op jit(solution)/shard_map/all_to_all | solution.py:37
  119.3 0.1 mul.81
  119.5 0.0 copy-done.2
  119.5 0.1 copy.24
  119.6 50.9 %all-to-all-done.1 = bf16[128,4,4096]{2,1,0:T(4,128)(2,1)} async-done(((bf16[128,4,4096]{2,1,0:T(4,128)(2,1)}), bf16[128,4,4096]{2,1,0:T(4,128)(2,1)}, u32[]{:S(2)}, u32[]{:S(2)}) %all-to-all-start.1) | async-done | bytes 4194336 | tf_op jit(solution)/shard_map/all_to_all | solution.py:37
  170.5 6.9 %reshape.80 = bf16[512,4096]{1,0:T(8,128)(2,1)} reshape(bf16[128,4,4096]{2,1,0:T(4,128)(2,1)} %all-to-all-done.1) | data formatting | bytes 8388608 | tf_op jit(solution)/shard_map/reshape | solution.py:52
  177.4 11.0 %gather_fusion = bf16[384,4096]{1,0:T(8,128)(2,1)} fusion(bf16[512,4096]{1,0:T(8,128)(2,1)} %reshape.80, s32[1024]{0:T(1024)S(1)} %pad_clamp_fusion), kind=kCustom, calls=%fused_computation | custom fusion | bytes 6292992 | tf_op jit(solution)/shard_map/gather | solution.py:53
  188.4 6.1 %reshape.81 = f32[64,6,4096]{2,1,0:T(8,128)} reshape(bf16[384,4096]{1,0:T(8,128)(2,1)} %gather_fusion) | data formatting | bytes 9437184 | tf_op jit(solution)/shard_map/convert_element_type | solution.py:53
  194.5 7.3 %multiply_reduce_fusion = bf16[64,4096]{1,0:T(8,128)(2,1)} fusion(f32[64,6,4096]{2,1,0:T(8,128)} %reshape.81, f32[64,6]{1,0:T(8,128)S(1)} %copy.24), kind=kLoop, calls=%fused_computation.1 | loop fusion | flops 2883584 | bytes 6817280 | tf_op jit(solution)/shard_map/reduce_sum | solution.py:54
  (14 shorter events, 0.1 us)
Async XLA Ops:
  0.0 2.2 %copy-start = (bf16[64,4096]{1,0:T(8,128)(2,1)S(1)}, bf16[64,4096]{1,0:T(8,128)(2,1)}, u32[]{:S(2)}) copy-start(bf16[64,4096]{1,0:T(8,128)(2,1)} %param.9) | copy-start | bytes 1572868
  12.6 12.0 %copy-start.3 = (f32[1,768]{1,0:T(1,128)S(1)}, f32[1,768]{1,0:T(1,128)}, u32[]{:S(2)}) copy-start(f32[1,768]{1,0:T(1,128)} %param.15) | copy-start | bytes 9220
  12.6 12.0 %copy-start.4 = (f32[1,768]{1,0:T(1,128)S(1)}, f32[1,768]{1,0:T(1,128)}, u32[]{:S(2)}) copy-start(f32[1,768]{1,0:T(1,128)} %param.16) | copy-start | bytes 9220
  12.6 63.1 %all-to-all-start = ((bf16[128,4,4096]{2,1,0:T(4,128)(2,1)}), bf16[128,4,4096]{2,1,0:T(4,128)(2,1)}, u32[]{:S(2)}, u32[]{:S(2)}) async-start(bf16[128,4,4096]{2,1,0:T(4,128)(2,1)} %reshape.77), calls=%async_computation | async-start | bytes 8388608 | tf_op jit(solution)/shard_map/all_to_all | solution.py:39
  82.6 7.1 %copy-start.5 = (f32[1,4096]{1,0:T(1,128)S(1)}, f32[1,4096]{1,0:T(1,128)}, u32[]{:S(2)}) copy-start(f32[1,4096]{1,0:T(1,128)} %param.17) | copy-start | bytes 49156
  113.5 6.0 %copy-start.2 = (f32[64,6]{0,1:T(8,128)S(1)}, f32[64,6]{0,1:T(8,128)}, u32[]{:S(2)}) copy-start(f32[64,6]{0,1:T(8,128)} %param.11) | copy-start | bytes 4612
  113.5 57.0 %all-to-all-start.1 = ((bf16[128,4,4096]{2,1,0:T(4,128)(2,1)}), bf16[128,4,4096]{2,1,0:T(4,128)(2,1)}, u32[]{:S(2)}, u32[]{:S(2)}) async-start(bf16[128,4,4096]{2,1,0:T(4,128)(2,1)} %reshape.79), calls=%async_computation.1 | async-start | bytes 8388608 | tf_op jit(solution)/shard_map/all_to_all | solution.py:37
  188.4 13.4 %copy-start.1 = (bf16[64,4096]{1,0:T(8,128)(2,1)S(1)}, bf16[64,4096]{1,0:T(8,128)(2,1)}, u32[]{:S(2)}) copy-start(bf16[64,4096]{1,0:T(8,128)(2,1)} %param.9) | copy-start | bytes 1572868
where the time goes:
time: 203 us; the launch traced here: 202 us
  waiting for transfers between devices  102 us (50%)
  local copies, waits for them, and re-layouts  47 us (23%)
  matrix products  26.9 us (13%)
  starting transfers between devices  17.8 us (9%)
  other arithmetic  8.07 us (4%)
    all_to_all x1, waiting for transfers between devices, on_device(): lax.all_to_all(packed, ('node', 'wide'), split_axis=0, concat_axis=0, til...  51.1 us
    all_to_all x1, waiting for transfers between devices, on_device(): lax.all_to_all(expert_block(lax.all_to_all(packed, ('node', 'wide'), spli...  50.9 us
    dot_general x1, matrix products, expert_block(): jnp.dot(hidden, w_down[0], preferred_element_type=jnp.float32)  16.6 us
    all_to_all x1, starting transfers between devices, on_device(): lax.all_to_all(packed, ('node', 'wide'), split_axis=0, concat_axis=0, til...  11.9 us
    gather x1, local copies, waits for them, and re-layouts, on_device(): chosen = results[slots].reshape(count, top, width).astype(jnp.float32)  11 us
    reduce_sum x1, other arithmetic, on_device(): mixed = jnp.sum(chosen * gate_weights[:, :, None], axis=1)  7.33 us
    reshape x1, local copies, waits for them, and re-layouts, on_device(): packed = packed.astype(jnp.bfloat16).reshape(experts, capacity, width)  7.19 us
    reshape x1, local copies, waits for them, and re-layouts, expert_block(): return routed.astype(jnp.bfloat16).reshape(shape)  7.19 us
  transfers between devices with their start and end apart: 2, of which 2 were waited for; matrix products, arithmetic and copies ran while one was open for 0% of the time, Pallas kernels for 0%

commit v1 on v0

v1 whole, which is shorter than its diff:
```python
import functools

import jax
import jax.numpy as jnp
from jax import lax
from jax.experimental import pallas as pl
from jax.experimental.pallas import tpu as pltpu
from jax.sharding import PartitionSpec as P

AXES = ("node", "wide")
BF = jnp.bfloat16
F32 = jnp.float32
MIB = 1 << 20


def iota(shape, dim):
    return lax.broadcasted_iota(jnp.int32, shape, dim)


def onehot(mask):
    return jnp.where(mask, 1.0, 0.0).astype(BF)


def dot(a, b, dims=((1,), (0,))):
    return lax.dot_general(a, b, (dims, ((), ())), preferred_element_type=F32)


def codes(ids, experts):
    top, count = ids.shape
    named = jnp.zeros((experts, count), F32)
    for k in range(top):
        named = named + jnp.where(iota((experts, count), 0) == ids[k : k + 1, :], 1.0, 0.0)
    named = named.astype(BF)
    lane = iota((count, 2 * count), 1) % count
    row = iota((count, 2 * count), 0)
    position = dot(named, onehot(row < lane))
    twice = dot(named, onehot(row == lane))
    return (position + 8.0 * (1.0 - twice)).astype(BF)


def pack_body(ids_ref, low_ref, high_ref, out_ref, hot_ref, *, experts, slots):
    count = low_ref.shape[0]
    rows = experts * 2 * slots

    @pl.when(pl.program_id(0) == 0)
    def _():
        code = codes(ids_ref[...], experts)
        spread = onehot(iota((rows, experts), 0) // (2 * slots) == iota((rows, experts), 1))
        wide = dot(spread, code)
        shape = (rows, 2 * count)
        slot = (iota(shape, 0) % slots).astype(F32)
        half = iota(shape, 0) // slots % 2
        hot_ref[...] = onehot((wide == slot) & (half == iota(shape, 1) // count))

    stacked = jnp.concatenate([low_ref[...], high_ref[...]], axis=0)
    out_ref[...] = dot(hot_ref[...], stacked).astype(BF)


def pack(ids, tokens, experts, slots, steps=4):
    top, count = ids.shape
    half = tokens.shape[1] // 2
    width = half // steps
    rows = experts * 2 * slots
    return pl.pallas_call(
        functools.partial(pack_body, experts=experts, slots=slots),
        out_shape=jax.ShapeDtypeStruct((rows, half), BF),
        grid=(steps,),
        in_specs=[
            pl.BlockSpec((top, count), lambda i: (0, 0)),
            pl.BlockSpec((count, width), lambda i: (0, i)),
            pl.BlockSpec((count, width), lambda i: (0, i + steps)),
        ],
        out_specs=pl.BlockSpec((rows, width), lambda i: (0, i)),
        scratch_shapes=[pltpu.VMEM((rows, 2 * count), BF)],
        compiler_params=pltpu.CompilerParams(vmem_limit_bytes=24 * MIB),
        name="pack",
    )(ids, tokens, tokens)


def mixer_body(ids_ref, weights_ref, out_ref, *, experts, slots):
    ids, weights = ids_ref[...], weights_ref[...]
    top, count = ids.shape
    rows = experts * 2 * slots
    code = codes(ids, experts)
    chosen = jnp.zeros((experts, count), F32)
    for k in range(top):
        chosen = chosen + jnp.where(iota((experts, count), 0) == ids[k : k + 1, :], weights[k : k + 1, :], 0.0)
    twice = onehot(iota((count, 2 * count), 0) == iota((count, 2 * count), 1) % count)
    spread = onehot(iota((experts, rows), 1) // (2 * slots) == iota((experts, rows), 0))
    shape = (2 * count, rows)
    wide = dot(code, spread, ((0,), (0,)))
    slot = (iota(shape, 1) % slots).astype(F32)
    here = (wide == slot) & (iota(shape, 1) // slots % 2 == iota(shape, 0) // count)
    high = chosen.astype(BF)
    low = (chosen - high.astype(F32)).astype(BF)
    for n, part in enumerate((high, low)):
        part = dot(part, twice).astype(BF)
        part = dot(part, spread, ((0,), (0,)))
        out_ref[n * 2 * count : (n + 1) * 2 * count, :] = jnp.where(here, part, 0.0).astype(BF)


def mixer(ids, weights, experts, slots):
    count = ids.shape[1]
    return pl.pallas_call(
        functools.partial(mixer_body, experts=experts, slots=slots),
        out_shape=jax.ShapeDtypeStruct((4 * count, experts * 2 * slots), BF),
        compiler_params=pltpu.CompilerParams(vmem_limit_bytes=24 * MIB),
        name="mixer",
    )(ids, weights)


def expert_body(
    x_hbm, gate_hbm, up_hbm, down_hbm, gate_s, up_s, down_s, out_hbm,
    x_buf, g_buf, u_buf, d_buf, xs, hid, o_buf, x_sem, g_sem, u_sem, d_sem, o_sem,
    *, slots, nb, cb,
):
    rows, half = x_hbm.shape
    ffw = gate_s.shape[1]
    wn, wc = ffw // nb, half // cb
    blocks = rows // 256

    def copies():
        xc = [pltpu.make_async_copy(x_hbm.at[pl.ds(b * 256, 256)], x_buf.at[pl.ds(b * 256, 256)], x_sem.at[b]) for b in range(blocks)]
        gc = [pltpu.make_async_copy(gate_hbm.at[0, :, pl.ds(n * wn, wn)], g_buf.at[n], g_sem.at[n]) for n in range(nb)]
        uc = [pltpu.make_async_copy(up_hbm.at[0, :, pl.ds(n * wn, wn)], u_buf.at[n], u_sem.at[n]) for n in range(nb)]
        dc = [pltpu.make_async_copy(down_hbm.at[0, :, pl.ds(c * wc, wc)], d_buf.at[c], d_sem.at[c]) for c in range(2 * cb)]
        return xc, gc, uc, dc

    xc, gc, uc, dc = copies()
    for c in xc:
        c.start()
    for n in range(nb):
        gc[n].start()
        uc[n].start()
    for c in range(cb):
        dc[c].start()
        dc[cb + c].start()

    a, b = iota((256, 256), 0), iota((256, 256), 1)
    split = onehot(b == a % 128 // slots * (2 * slots) + a // 128 * slots + a % slots)
    join = onehot(a == b % 128 // slots * (2 * slots) + b // 128 * slots + b % slots)

    for n in range(blocks):
        xc[n].wait()
        part = dot(split, x_buf[n * 256 : (n + 1) * 256, :]).astype(BF)
        xs[n * 128 : (n + 1) * 128, :half] = part[:128]
        xs[n * 128 : (n + 1) * 128, half:] = part[128:]
    for n in range(nb):
        gc[n].wait()
        gate = dot(xs[...], g_buf[n]) * gate_s[:, n * wn : (n + 1) * wn]
        uc[n].wait()
        up = dot(xs[...], u_buf[n]) * up_s[:, n * wn : (n + 1) * wn]
        hid[:, n * wn : (n + 1) * wn] = (gate / (1.0 + jnp.exp(-gate)) * up).astype(BF)
    for c in range(cb):
        dc[c].wait()
        dc[cb + c].wait()
        low = (dot(hid[...], d_buf[c]) * down_s[:, c * wc : (c + 1) * wc]).astype(BF)
        high = (dot(hid[...], d_buf[cb + c]) * down_s[:, half + c * wc : half + (c + 1) * wc]).astype(BF)
        for n in range(blocks):
            both = jnp.concatenate([low[n * 128 : (n + 1) * 128], high[n * 128 : (n + 1) * 128]], axis=0)
            o_buf[c, n * 256 : (n + 1) * 256, :] = dot(join, both).astype(BF)
        pltpu.make_async_copy(o_buf.at[c], out_hbm.at[:, pl.ds(c * wc, wc)], o_sem.at[c]).start()
    for c in range(cb):
        pltpu.make_async_copy(o_buf.at[c], out_hbm.at[:, pl.ds(c * wc, wc)], o_sem.at[c]).wait()


def expert(x, w_gate, w_up, w_down, gate_scale, up_scale, down_scale, slots, nb=3, cb=4):
    rows, half = x.shape
    width, ffw = w_gate.shape[1:]
    wn, wc = ffw // nb, half // cb
    whole = pl.BlockSpec(memory_space=pltpu.VMEM)
    hbm = pl.BlockSpec(memory_space=pl.ANY)
    return pl.pallas_call(
        functools.partial(expert_body, slots=slots, nb=nb, cb=cb),
        out_shape=jax.ShapeDtypeStruct((rows, half), BF),
        in_specs=[hbm, hbm, hbm, hbm, whole, whole, whole],
        out_specs=hbm,
        scratch_shapes=[
            pltpu.VMEM((rows, half), BF),
            pltpu.VMEM((nb, width, wn), BF),
            pltpu.VMEM((nb, width, wn), BF),
            pltpu.VMEM((2 * cb, ffw, wc), BF),
            pltpu.VMEM((rows // 2, width), BF),
            pltpu.VMEM((rows // 2, ffw), BF),
            pltpu.VMEM((cb, rows, wc), BF),
            pltpu.SemaphoreType.DMA((rows // 256,)),
            pltpu.SemaphoreType.DMA((nb,)),
            pltpu.SemaphoreType.DMA((nb,)),
            pltpu.SemaphoreType.DMA((2 * cb,)),
            pltpu.SemaphoreType.DMA((cb,)),
        ],
        compiler_params=pltpu.CompilerParams(vmem_limit_bytes=56 * MIB),
        name="expert",
    )(x, w_gate, w_up, w_down, gate_scale, up_scale, down_scale)


def mix_body(w_ref, r_ref, out_ref, *, steps):
    count = w_ref.shape[0] // 4
    half = out_ref.shape[1] // 2
    width = half // steps
    both = dot(w_ref[...], r_ref[...])
    total = (both[: 2 * count] + both[2 * count :]).astype(BF)
    at = pl.multiple_of(pl.program_id(0) * width, width)
    out_ref[:, pl.ds(at, width)] = total[:count]
    out_ref[:, pl.ds(half + at, width)] = total[count:]


def mix(weights, results, steps=4):
    count = weights.shape[0] // 4
    rows, half = results.shape
    width = half // steps
    return pl.pallas_call(
        functools.partial(mix_body, steps=steps),
        out_shape=jax.ShapeDtypeStruct((count, 2 * half), BF),
        grid=(steps,),
        in_specs=[
            pl.BlockSpec(weights.shape, lambda i: (0, 0)),
            pl.BlockSpec((rows, width), lambda i: (0, i)),
        ],
        out_specs=pl.BlockSpec((count, 2 * half), lambda i: (0, 0)),
        compiler_params=pltpu.CompilerParams(vmem_limit_bytes=24 * MIB),
        name="mix",
    )(weights, results)


def exchange(x, experts):
    rows, width = x.shape
    x = x.reshape(experts, rows // experts, width)
    return lax.all_to_all(x, AXES, split_axis=0, concat_axis=0, tiled=True).reshape(rows, width)


def on_device(tokens, expert_ids, gate_weights, w_gate, w_up, w_down, gate_scale, up_scale, down_scale):
    experts = lax.axis_size(AXES)
    slots = 4
    ids, weights = expert_ids.T, gate_weights.T
    packed = pack(ids, tokens, experts, slots)
    received = exchange(packed, experts)
    routed = expert(received, w_gate, w_up, w_down, gate_scale, up_scale, down_scale, slots)
    returned = exchange(routed, experts)
    return mix(mixer(ids, weights, experts, slots), returned)


def solution(mesh):
    row = P(AXES, None)
    placed = (row, row, row, P(AXES, None, None), P(AXES, None, None), P(AXES, None, None), row, row, row)
    return jax.shard_map(on_device, mesh=mesh, in_specs=placed, out_specs=row, check_vma=False)
```

time: 203 us -> 157 us (0.77)
  blocking collectives: 0 us -> 62.9 us
  waiting for transfers between devices: 102 us -> 50.2 us
  local copies, waits for them, and re-layouts: 47 us -> 1.74 us
  Pallas kernels: 0 us -> 35.8 us
  matrix products: 26.9 us -> 0 us
  starting transfers between devices: 17.8 us -> 5.83 us
  other arithmetic: 8.07 us -> 0 us
    all_to_all x0 -> x1, blocking collectives: none -> 62.9 us  [exchange(): lax.all_to_all(x, AXES, split_axis=0, concat_axis=0, tiled=True)]
    all_to_all x2 -> x1, waiting for transfers between devices: 102 us -> 50.2 us  [exchange(): lax.all_to_all(x, AXES, split_axis=0, concat_axis=0, tiled=True)]
    pallas_call x0 -> x4, Pallas kernels: none -> 35.8 us  [the longest x1 27.7 us: expert(): pl.pallas_call(functools.partial(expert_body, slots=slots, nb=nb, cb=cb),...]
    reshape x4 -> x0, local copies, waits for them, and re-layouts: 28.2 us -> none  [the longest x1 7.19 us: on_device(): packed = packed.astype(jnp.bfloat16).reshape(experts, capacity, width)]
    dot_general x3 -> x0, matrix products: 26.9 us -> none  [the longest x1 16.6 us: expert_block(): jnp.dot(hidden, w_down[0], preferred_element_type=jnp.float32)]
    all_to_all x2 -> x1, starting transfers between devices: 17.8 us -> 5.83 us  [exchange(): lax.all_to_all(x, AXES, split_axis=0, concat_axis=0, tiled=True)]
    gather x1 -> x0, local copies, waits for them, and re-layouts: 11 us -> none  [on_device(): chosen = results[slots].reshape(count, top, width).astype(jnp.float32)]
    reduce_sum x3 -> x0, other arithmetic: 7.71 us -> none  [the longest x1 7.33 us: on_device(): mixed = jnp.sum(chosen * gate_weights[:, :, None], axis=1)]
  transfers between devices with their start and end apart: 2 -> 1, of which waited for: 2 -> 1; matrix products, arithmetic and copies ran while one was open for 0% -> 0% of each run, Pallas kernels for 0% -> 1%
where the time goes in v1:
time: 157 us
  blocking collectives  62.9 us (40%)
  waiting for transfers between devices  50.2 us (32%)
  Pallas kernels  35.8 us (23%)
  starting transfers between devices  5.83 us (4%)
  local copies, waits for them, and re-layouts  1.74 us (1%)
    all_to_all x1, blocking collectives, exchange(): lax.all_to_all(x, AXES, split_axis=0, concat_axis=0, tiled=True)  62.9 us
    all_to_all x1, waiting for transfers between devices, exchange(): lax.all_to_all(x, AXES, split_axis=0, concat_axis=0, tiled=True)  50.2 us
    pallas_call x1, Pallas kernels, expert(): pl.pallas_call(functools.partial(expert_body, slots=slots, nb=nb, cb=cb),...  27.7 us
    all_to_all x1, starting transfers between devices, exchange(): lax.all_to_all(x, AXES, split_axis=0, concat_axis=0, tiled=True)  5.83 us
    pallas_call x1, Pallas kernels, mix(): pl.pallas_call(functools.partial(mix_body, steps=steps), out_shape=jax.Sh...  4.65 us
  transfers between devices with their start and end apart: 1, of which 1 were waited for; matrix products, arithmetic and copies ran while one was open for 0% of the time, Pallas kernels for 1%

profile of v1, /device:TPU:1, one launch (start us, length us, event | category | flops | bytes accessed | tf_op | source)
XLA Modules:
  0.0 156.5 jit_solution(7811136731465071175)
XLA Ops:
  0.0 0.0 copy-start
  0.0 1.0 copy-done
  1.0 0.0 copy-start.1
  1.0 0.7 copy-done.1
  1.7 2.5 %pack.1 = bf16[1024,2048]{1,0:T(8,128)(2,1)S(1)} custom-call(s32[6,64]{1,0:T(8,128)S(1)} %bitcast.7, bf16[64,4096]{1,0:T(8,128)(2,1)S(1)} %copy-done, bf16[64,4096]{1,0:T(8,128)(2,1)S(1)} %copy-done), custom_call_target="tpu_custom_call" | custom-call | tf_op jit(solution)/shard_map/pack/pallas_call | solution.py:64
  4.2 62.9 %all_to_all.10 = bf16[128,8,2048]{2,1,0:T(8,128)(2,1)} all-to-all(bf16[128,8,2048]{2,1,0:T(8,128)(2,1)S(1)} %bitcast.6), channel_id=1, replica_groups=mesh['node'=4,'wide'=32] {'node','wide'}, dimensions={0} | all-to-all | bytes 8388608 | tf_op jit(solution)/shard_map/all_to_all | solution.py:229
  67.1 27.7 %expert.1 = bf16[1024,2048]{1,0:T(8,128)(2,1)} custom-call(bf16[1024,2048]{1,0:T(8,128)(2,1)} %bitcast.11, bf16[1,4096,768]{2,1,0:T(8,128)(2,1)} %gate_hbm.1, bf16[1,4096,768]{2,1,0:T(8,128)(2,1)} %up_hbm.1, bf16[1,768,4096]{2,1,0:T(8,128)(2,1)} %down_hbm.1, f32[1,768]{1,0:T(1,128)} %gate_s.1, f32[1,768]{1,0:T(1,128)} %up_s.1, f32[1,4096]{1,0:T(1,128)} %down_s.1), custom_call_target="tpu_custom_call" | custom-call | tf_op jit(solution)/shard_map/expert/pallas_call | solution.py:173
  94.8 0.0 copy-start.2
  94.8 0.0 copy-start.3
  94.9 5.8 %all-to-all-start.1 = ((bf16[128,8,2048]{2,1,0:T(8,128)(2,1)}), bf16[128,8,2048]{2,1,0:T(8,128)(2,1)}, u32[]{:S(2)}, u32[]{:S(2)}) async-start(bf16[128,8,2048]{2,1,0:T(8,128)(2,1)} %bitcast.10), calls=%async_computation.1 | async-start | bytes 8388608 | tf_op jit(solution)/shard_map/all_to_all | solution.py:229
  100.7 0.0 copy-done.2
  100.7 0.0 copy-done.3
  100.7 0.9 mixer.1.w_ref
  101.7 50.2 %all-to-all-done.1 = bf16[128,8,2048]{2,1,0:T(8,128)(2,1)} async-done(((bf16[128,8,2048]{2,1,0:T(8,128)(2,1)}), bf16[128,8,2048]{2,1,0:T(8,128)(2,1)}, u32[]{:S(2)}, u32[]{:S(2)}) %all-to-all-start.1) | async-done | bytes 4194336 | tf_op jit(solution)/shard_map/all_to_all | solution.py:229
  151.9 4.6 %mix.1 = bf16[64,4096]{1,0:T(8,128)(2,1)} custom-call(bf16[256,1024]{1,0:T(8,128)(2,1)S(1)} %mixer.1.w_ref, bf16[1024,2048]{1,0:T(8,128)(2,1)} %bitcast.5.r_ref), custom_call_target="tpu_custom_call" | custom-call | tf_op jit(solution)/shard_map/mix/pallas_call | solution.py:212
Async XLA Ops:
  0.0 1.0 copy-start
  1.0 0.7 copy-start.1
  94.8 5.9 %copy-start.2 = (s32[64,6]{0,1:T(8,128)S(1)}, s32[64,6]{0,1:T(8,128)}, u32[]{:S(2)}) copy-start(s32[64,6]{0,1:T(8,128)} %param.10) | copy-start | bytes 4612
  94.8 5.9 %copy-start.3 = (f32[64,6]{0,1:T(8,128)S(1)}, f32[64,6]{0,1:T(8,128)}, u32[]{:S(2)}) copy-start(f32[64,6]{0,1:T(8,128)} %param.11) | copy-start | bytes 4612
  94.9 57.0 %all-to-all-start.1 = ((bf16[128,8,2048]{2,1,0:T(8,128)(2,1)}), bf16[128,8,2048]{2,1,0:T(8,128)(2,1)}, u32[]{:S(2)}, u32[]{:S(2)}) async-start(bf16[128,8,2048]{2,1,0:T(8,128)(2,1)} %bitcast.10), calls=%async_computation.1 | async-start | bytes 8388608 | tf_op jit(solution)/shard_map/all_to_all | solution.py:229

commit v2 on v1

v2 whole, which is shorter than its diff:
```python
import functools

import jax
import jax.numpy as jnp
from jax import lax
from jax.experimental import pallas as pl
from jax.experimental.pallas import tpu as pltpu
from jax.sharding import PartitionSpec as P

AXES = ("node", "wide")
BF = jnp.bfloat16
F32 = jnp.float32
MIB = 1 << 20


def iota(shape, dim):
    return lax.broadcasted_iota(jnp.int32, shape, dim)


def onehot(mask):
    return jnp.where(mask, 1.0, 0.0).astype(BF)


def dot(a, b, dims=((1,), (0,))):
    return lax.dot_general(a, b, (dims, ((), ())), preferred_element_type=F32)


def in_hbm(x):
    return pltpu.with_memory_space_constraint(x, pltpu.HBM)


def codes(ids, experts):
    top, count = ids.shape
    named = jnp.zeros((experts, count), F32)
    for k in range(top):
        named = named + jnp.where(iota((experts, count), 0) == ids[k : k + 1, :], 1.0, 0.0)
    named = named.astype(BF)
    lane = iota((count, 2 * count), 1) % count
    row = iota((count, 2 * count), 0)
    position = dot(named, onehot(row < lane))
    twice = dot(named, onehot(row == lane))
    return (position + 8.0 * (1.0 - twice)).astype(BF)


def pack_body(ids_hbm, tokens_hbm, out_ref, ids_ref, tok_ref, sem, *, experts, slots, steps):
    count, width = tok_ref.shape
    half = width // 2
    rows = experts * 2 * slots
    ids_copy = pltpu.make_async_copy(ids_hbm, ids_ref, sem.at[0])
    tok_copy = pltpu.make_async_copy(tokens_hbm, tok_ref, sem.at[1])
    ids_copy.start()
    tok_copy.start()
    shape = (rows, 2 * count)
    spread = onehot(iota((rows, experts), 0) // (2 * slots) == iota((rows, experts), 1))
    slot = (iota(shape, 0) % slots).astype(F32)
    half_of = iota(shape, 0) // slots % 2 == iota(shape, 1) // count
    ids_copy.wait()
    wide = dot(spread, codes(ids_ref[...], experts))
    hot = onehot((wide == slot) & half_of)
    tok_copy.wait()
    step = half // steps
    for n in range(steps):
        at = slice(n * step, (n + 1) * step)
        stacked = jnp.concatenate([tok_ref[:, at], tok_ref[:, half + n * step : half + (n + 1) * step]], axis=0)
        out_ref[:, at] = dot(hot, stacked).astype(BF)


def pack(ids, tokens, experts, slots, steps=4):
    rows = experts * 2 * slots
    hbm = pl.BlockSpec(memory_space=pltpu.HBM)
    return pl.pallas_call(
        functools.partial(pack_body, experts=experts, slots=slots, steps=steps),
        out_shape=jax.ShapeDtypeStruct((rows, tokens.shape[1] // 2), BF),
        in_specs=[hbm, hbm],
        out_specs=pl.BlockSpec(memory_space=pltpu.VMEM),
        scratch_shapes=[
            pltpu.VMEM(ids.shape, jnp.int32),
            pltpu.VMEM(tokens.shape, BF),
            pltpu.SemaphoreType.DMA((2,)),
        ],
        compiler_params=pltpu.CompilerParams(vmem_limit_bytes=12 * MIB),
        name="pack",
    )(in_hbm(ids), in_hbm(tokens))


def mixer_body(ids_ref, weights_ref, out_ref, *, experts, slots):
    ids, weights = ids_ref[...], weights_ref[...]
    top, count = ids.shape
    rows = experts * 2 * slots
    code = codes(ids, experts)
    chosen = jnp.zeros((experts, count), F32)
    for k in range(top):
        chosen = chosen + jnp.where(iota((experts, count), 0) == ids[k : k + 1, :], weights[k : k + 1, :], 0.0)
    twice = onehot(iota((count, 2 * count), 0) == iota((count, 2 * count), 1) % count)
    spread = onehot(iota((experts, rows), 1) // (2 * slots) == iota((experts, rows), 0))
    shape = (2 * count, rows)
    wide = dot(code, spread, ((0,), (0,)))
    slot = (iota(shape, 1) % slots).astype(F32)
    here = (wide == slot) & (iota(shape, 1) // slots % 2 == iota(shape, 0) // count)
    high = chosen.astype(BF)
    low = (chosen - high.astype(F32)).astype(BF)
    for n, part in enumerate((high, low)):
        part = dot(part, twice).astype(BF)
        part = dot(part, spread, ((0,), (0,)))
        out_ref[n * 2 * count : (n + 1) * 2 * count, :] = jnp.where(here, part, 0.0).astype(BF)


def mixer(ids, weights, experts, slots):
    count = ids.shape[1]
    return pl.pallas_call(
        functools.partial(mixer_body, experts=experts, slots=slots),
        out_shape=jax.ShapeDtypeStruct((4 * count, experts * 2 * slots), BF),
        compiler_params=pltpu.CompilerParams(vmem_limit_bytes=8 * MIB),
        name="mixer",
    )(ids, weights)


def swap(first, second):
    top = iota(first.shape, 1) < 4
    return (
        jnp.where(top, first, pltpu.roll(second, 4, 1)),
        jnp.where(top, pltpu.roll(first, 4, 1), second),
    )


def expert_body(
    x_ref, gate_ref, up_ref, down_hbm, gate_s, up_s, down_s, out_hbm, d_buf, xs, hid, o_buf, d_sem, o_sem, *, slots, nb, cb
):
    rows, half = x_ref.shape
    ffw = gate_s.shape[1]
    wn, wc = ffw // nb, half // cb
    blocks = rows // 256
    downs = [pltpu.make_async_copy(down_hbm.at[0, pl.ds(n * wn, wn)], d_buf.at[pl.ds(n * wn, wn)], d_sem.at[n]) for n in range(nb)]
    outs = [pltpu.make_async_copy(o_buf.at[:, pl.ds(c * wc, wc)], out_hbm.at[:, pl.ds(c * wc, wc)], o_sem.at[c]) for c in range(cb)]
    for copy in downs:
        copy.start()
    wx = 256
    for n in range(half // wx):
        at = slice(n * wx, (n + 1) * wx)
        pairs = x_ref[:, at].astype(F32).reshape(rows // 16, 2, 8, wx)
        low, high = swap(pairs[:, 0], pairs[:, 1])
        xs[:, at] = low.reshape(rows // 2, wx).astype(BF)
        xs[:, half + n * wx : half + (n + 1) * wx] = high.reshape(rows // 2, wx).astype(BF)
    for n in range(nb):
        at = slice(n * wn, (n + 1) * wn)
        gate = dot(xs[...], gate_ref[0, :, at]) * gate_s[:, at]
        up = dot(xs[...], up_ref[0, :, at]) * up_s[:, at]
        hid[:, at] = (gate / (1.0 + jnp.exp(-gate)) * up).astype(BF)
    for copy in downs:
        copy.wait()
    for c in range(cb):
        at, to = slice(c * wc, (c + 1) * wc), slice(half + c * wc, half + (c + 1) * wc)
        low = dot(hid[...], d_buf[:, at]) * down_s[:, at]
        high = dot(hid[...], d_buf[:, to]) * down_s[:, to]
        tile = (rows // 16, 8, wc)
        even, odd = swap(low.reshape(tile), high.reshape(tile))
        both = jnp.concatenate([even[:, None], odd[:, None]], axis=1)
        o_buf[:, at] = both.reshape(rows, wc).astype(BF)
        outs[c].start()
    for copy in outs:
        copy.wait()


def expert(x, w_gate, w_up, w_down, gate_scale, up_scale, down_scale, slots, nb=3, cb=4):
    rows, half = x.shape
    width, ffw = w_gate.shape[1:]
    whole = pl.BlockSpec(memory_space=pltpu.VMEM)
    hbm = pl.BlockSpec(memory_space=pltpu.HBM)
    return pl.pallas_call(
        functools.partial(expert_body, slots=slots, nb=nb, cb=cb),
        out_shape=pltpu.HBM((rows, half), BF),
        in_specs=[whole, whole, whole, hbm, whole, whole, whole],
        out_specs=hbm,
        scratch_shapes=[
            pltpu.VMEM((ffw, width), BF),
            pltpu.VMEM((rows // 2, width), BF),
            pltpu.VMEM((rows // 2, ffw), BF),
            pltpu.VMEM((rows, half), BF),
            pltpu.SemaphoreType.DMA((nb,)),
            pltpu.SemaphoreType.DMA((cb,)),
        ],
        compiler_params=pltpu.CompilerParams(vmem_limit_bytes=24 * MIB),
        name="expert",
    )(x, w_gate, w_up, in_hbm(w_down), gate_scale, up_scale, down_scale)


def mix_body(w_ref, r_hbm, out_hbm, r_buf, buf, in_sem, sem, *, steps):
    count = w_ref.shape[0] // 4
    half = r_buf.shape[1]
    step = half // steps
    here = [pl.ds(n * step, step) for n in range(2 * steps)]
    loads = [pltpu.make_async_copy(r_hbm.at[:, here[n]], r_buf.at[:, here[n]], in_sem.at[n]) for n in range(steps)]
    stores = [pltpu.make_async_copy(buf.at[:, here[n]], out_hbm.at[:, here[n]], sem.at[n]) for n in range(2 * steps)]
    for copy in loads:
        copy.start()
    for n in range(steps):
        loads[n].wait()
        both = dot(w_ref[...], r_buf[:, n * step : (n + 1) * step])
        total = (both[: 2 * count] + both[2 * count :]).astype(BF)
        for h in range(2):
            at = h * half + n * step
            buf[:, at : at + step] = total[h * count : (h + 1) * count]
            stores[h * steps + n].start()
    for copy in stores:
        copy.wait()


def mix(weights, results, steps=4):
    count = weights.shape[0] // 4
    rows, half = results.shape
    hbm = pl.BlockSpec(memory_space=pltpu.HBM)
    return pl.pallas_call(
        functools.partial(mix_body, steps=steps),
        out_shape=jax.ShapeDtypeStruct((count, 2 * half), BF),
        in_specs=[pl.BlockSpec(memory_space=pltpu.VMEM), hbm],
        out_specs=hbm,
        scratch_shapes=[
            pltpu.VMEM((rows, half), BF),
            pltpu.VMEM((count, 2 * half), BF),
            pltpu.SemaphoreType.DMA((steps,)),
            pltpu.SemaphoreType.DMA((2 * steps,)),
        ],
        compiler_params=pltpu.CompilerParams(vmem_limit_bytes=16 * MIB),
        name="mix",
    )(weights, results)


def exchange(x, experts):
    rows, width = x.shape
    x = x.reshape(experts, rows // experts, width)
    return lax.all_to_all(x, AXES, split_axis=0, concat_axis=0, tiled=True).reshape(rows, width)


def on_device(tokens, expert_ids, gate_weights, w_gate, w_up, w_down, gate_scale, up_scale, down_scale):
    experts = lax.axis_size(AXES)
    slots = 4
    ids, weights = expert_ids.T, gate_weights.T
    packed = pack(ids, tokens, experts, slots)
    received = exchange(packed, experts)
    routed = expert(received, w_gate, w_up, w_down, gate_scale, up_scale, down_scale, slots)
    returned = exchange(routed, experts)
    return mix(mixer(ids, weights, experts, slots), returned)


def solution(mesh):
    row = P(AXES, None)
    placed = (row, row, row, P(AXES, None, None), P(AXES, None, None), P(AXES, None, None), row, row, row)
    return jax.shard_map(on_device, mesh=mesh, in_specs=placed, out_specs=row, check_vma=False)
```

time: 157 us -> 140 us (0.89)
  Pallas kernels: 35.8 us -> 20.7 us
  local copies, waits for them, and re-layouts: 1.74 us -> 0.04 us
    pallas_call x1, Pallas kernels: 27.7 us -> 13.5 us  [expert(): pl.pallas_call(functools.partial(expert_body, slots=slots, nb=nb, cb=cb),...]
    unnamed x8 -> x16, local copies, waits for them, and re-layouts: 1.74 us -> 0.04 us
where the time goes in v2:
time: 140 us
  blocking collectives  62.8 us (45%)
  waiting for transfers between devices  50.2 us (36%)
  Pallas kernels  20.7 us (15%)
  starting transfers between devices  5.83 us (4%)
    all_to_all x1, blocking collectives, exchange(): lax.all_to_all(x, AXES, split_axis=0, concat_axis=0, tiled=True)  62.8 us
    all_to_all x1, waiting for transfers between devices, exchange(): lax.all_to_all(x, AXES, split_axis=0, concat_axis=0, tiled=True)  50.2 us
    pallas_call x1, Pallas kernels, expert(): pl.pallas_call(functools.partial(expert_body, slots=slots, nb=nb, cb=cb),...  13.5 us
    all_to_all x1, starting transfers between devices, exchange(): lax.all_to_all(x, AXES, split_axis=0, concat_axis=0, tiled=True)  5.83 us
    pallas_call x1, Pallas kernels, mix(): pl.pallas_call(functools.partial(mix_body, steps=steps), out_shape=jax.Sh...  3.75 us
  transfers between devices with their start and end apart: 1, of which 1 were waited for; matrix products, arithmetic and copies ran while one was open for 0% of the time, Pallas kernels for 1%

profile of v2, /device:TPU:1, one launch (start us, length us, event | category | flops | bytes accessed | tf_op | source)
XLA Modules:
  0.0 139.6 jit_solution(13621846887515272318)
XLA Ops:
  0.0 0.0 slice-start
  0.0 0.0 copy-start.2
  0.0 0.0 copy-start.4
  0.0 0.0 copy-start.5
  0.0 2.5 %pack.1 = bf16[1024,2048]{1,0:T(8,128)(2,1)S(1)} custom-call(s32[6,64]{1,0:T(8,128)} %bitcast.10, bf16[64,4096]{1,0:T(8,128)(2,1)} %tokens_hbm.1), custom_call_target="tpu_custom_call" | custom-call | tf_op jit(solution)/shard_map/pack/pallas_call | solution.py:71
  2.5 0.0 slice-start.1
  2.5 0.0 copy-start
  2.5 62.8 %all_to_all.10 = bf16[128,8,2048]{2,1,0:T(8,128)(2,1)S(1)} all-to-all(bf16[128,8,2048]{2,1,0:T(8,128)(2,1)S(1)} %bitcast.6), channel_id=1, replica_groups=mesh['node'=4,'wide'=32] {'node','wide'}, dimensions={0} | all-to-all | bytes 8388608 | tf_op jit(solution)/shard_map/all_to_all | solution.py:231
  65.3 0.0 slice-done
  65.3 0.0 copy-done.2
  65.3 0.0 copy-done.4
  65.4 0.0 copy-done.5
  65.4 0.0 slice-done.1
  65.4 0.0 copy-done
  65.4 13.5 %expert.1 = bf16[1024,2048]{1,0:T(8,128)(2,1)} custom-call(bf16[1024,2048]{1,0:T(8,128)(2,1)S(1)} %bitcast.7, bf16[1,4096,768]{2,1,0:T(8,128)(2,1)S(1)} %bitcast.9, bf16[1,4096,768]{2,1,0:T(8,128)(2,1)S(1)} %copy-done, bf16[1,768,4096]{2,1,0:T(8,128)(2,1)} %down_hbm.1, f32[1,768]{1,0:T(1,128)S(1)} %copy-done.4, f32[1,768]{1,0:T(1,128)S(1)} %copy-done.5, ...), custom_call_target="tpu_custom_call" | custom-call | tf_op jit(solution)/shard_map/expert/pallas_call | solution.py:169
  78.9 0.0 copy-start.1
  78.9 0.0 copy-start.3
  78.9 5.8 %all-to-all-start.1 = ((bf16[128,8,2048]{2,1,0:T(8,128)(2,1)}), bf16[128,8,2048]{2,1,0:T(8,128)(2,1)}, u32[]{:S(2)}, u32[]{:S(2)}) async-start(bf16[128,8,2048]{2,1,0:T(8,128)(2,1)} %bitcast.13), calls=%async_computation.1 | async-start | bytes 8388608 | tf_op jit(solution)/shard_map/all_to_all | solution.py:231
  84.7 0.0 copy-done.1
  84.7 0.0 copy-done.3
  84.8 0.9 mixer.1.w_ref
  85.7 50.2 %all-to-all-done.1 = bf16[128,8,2048]{2,1,0:T(8,128)(2,1)} async-done(((bf16[128,8,2048]{2,1,0:T(8,128)(2,1)}), bf16[128,8,2048]{2,1,0:T(8,128)(2,1)}, u32[]{:S(2)}, u32[]{:S(2)}) %all-to-all-start.1) | async-done | bytes 4194336 | tf_op jit(solution)/shard_map/all_to_all | solution.py:231
  135.9 3.8 %mix.1 = bf16[64,4096]{1,0:T(8,128)(2,1)} custom-call(bf16[256,1024]{1,0:T(8,128)(2,1)S(1)} %mixer.1.w_ref, bf16[1024,2048]{1,0:T(8,128)(2,1)} %bitcast.5.r_hbm), custom_call_target="tpu_custom_call" | custom-call | tf_op jit(solution)/shard_map/mix/pallas_call | solution.py:212
  (1 shorter events, 0.0 us)
Async XLA Ops:
  0.0 65.3 %slice-start = ((s8[6291456]{0:T(1024)(128)(4,1)}), s8[4194304]{0:T(1024)(128)(4,1)S(1)}, s32[]{:S(2)}) async-start(s8[6291456]{0:T(1024)(128)(4,1)} %bitcast.8), calls=%async_computation.2 | async-start | bytes 8388608
  0.0 65.3 %copy-start.2 = (f32[1,4096]{1,0:T(1,128)S(1)}, f32[1,4096]{1,0:T(1,128)}, u32[]{:S(2)}) copy-start(f32[1,4096]{1,0:T(1,128)} %down_s.1) | copy-start | bytes 49156
  0.0 65.3 %copy-start.4 = (f32[1,768]{1,0:T(1,128)S(1)}, f32[1,768]{1,0:T(1,128)}, u32[]{:S(2)}) copy-start(f32[1,768]{1,0:T(1,128)} %gate_s.1) | copy-start | bytes 9220
  0.0 65.3 %copy-start.5 = (f32[1,768]{1,0:T(1,128)S(1)}, f32[1,768]{1,0:T(1,128)}, u32[]{:S(2)}) copy-start(f32[1,768]{1,0:T(1,128)} %up_s.1) | copy-start | bytes 9220
  2.5 62.9 %slice-start.1 = ((s8[6291456]{0:T(1024)(128)(4,1)}), s8[2097152]{0:T(1024)(128)(4,1)S(1)}, s32[]{:S(2)}) async-start(s8[6291456]{0:T(1024)(128)(4,1)} %bitcast.8), calls=%async_computation.3 | async-start | bytes 4194304
  2.5 62.8 %copy-start = (bf16[1,4096,768]{2,1,0:T(8,128)(2,1)S(1)}, bf16[1,4096,768]{2,1,0:T(8,128)(2,1)}, u32[]{:S(2)}) copy-start(bf16[1,4096,768]{2,1,0:T(8,128)(2,1)} %up_ref.1) | copy-start | bytes 18874372
  78.9 5.9 %copy-start.1 = (s32[64,6]{0,1:T(8,128)S(1)}, s32[64,6]{0,1:T(8,128)}, u32[]{:S(2)}) copy-start(s32[64,6]{0,1:T(8,128)} %param.10) | copy-start | bytes 4612
  78.9 5.9 %copy-start.3 = (f32[64,6]{0,1:T(8,128)S(1)}, f32[64,6]{0,1:T(8,128)}, u32[]{:S(2)}) copy-start(f32[64,6]{0,1:T(8,128)} %param.11) | copy-start | bytes 4612
  78.9 57.0 %all-to-all-start.1 = ((bf16[128,8,2048]{2,1,0:T(8,128)(2,1)}), bf16[128,8,2048]{2,1,0:T(8,128)(2,1)}, u32[]{:S(2)}, u32[]{:S(2)}) async-start(bf16[128,8,2048]{2,1,0:T(8,128)(2,1)} %bitcast.13), calls=%async_computation.1 | async-start | bytes 8388608 | tf_op jit(solution)/shard_map/all_to_all | solution.py:231

commit v3 on v2

--- a/solution.py
+++ b/solution.py
@@ -83,8 +83,7 @@
     )(in_hbm(ids), in_hbm(tokens))
 
 
-def mixer_body(ids_ref, weights_ref, out_ref, *, experts, slots):
-    ids, weights = ids_ref[...], weights_ref[...]
+def table(ids, weights, experts, slots):
     top, count = ids.shape
     rows = experts * 2 * slots
     code = codes(ids, experts)
@@ -99,20 +98,12 @@
     here = (wide == slot) & (iota(shape, 1) // slots % 2 == iota(shape, 0) // count)
     high = chosen.astype(BF)
     low = (chosen - high.astype(F32)).astype(BF)
-    for n, part in enumerate((high, low)):
+    parts = []
+    for part in (high, low):
         part = dot(part, twice).astype(BF)
         part = dot(part, spread, ((0,), (0,)))
-        out_ref[n * 2 * count : (n + 1) * 2 * count, :] = jnp.where(here, part, 0.0).astype(BF)
-
-
-def mixer(ids, weights, experts, slots):
-    count = ids.shape[1]
-    return pl.pallas_call(
-        functools.partial(mixer_body, experts=experts, slots=slots),
-        out_shape=jax.ShapeDtypeStruct((4 * count, experts * 2 * slots), BF),
-        compiler_params=pltpu.CompilerParams(vmem_limit_bytes=8 * MIB),
-        name="mixer",
-    )(ids, weights)
+        parts.append(jnp.where(here, part, 0.0).astype(BF))
+    return jnp.concatenate(parts, axis=0)
 
 
 def swap(first, second):
@@ -124,14 +115,13 @@
 
 
 def expert_body(
-    x_ref, gate_ref, up_ref, down_hbm, gate_s, up_s, down_s, out_hbm, d_buf, xs, hid, o_buf, d_sem, o_sem, *, slots, nb, cb
+    x_ref, gate_ref, up_ref, down_hbm, gate_s, up_s, down_s, out_ref, d_buf, xs, hid, d_sem, *, slots, nb, cb
 ):
     rows, half = x_ref.shape
     ffw = gate_s.shape[1]
     wn, wc = ffw // nb, half // cb
     blocks = rows // 256
     downs = [pltpu.make_async_copy(down_hbm.at[0, pl.ds(n * wn, wn)], d_buf.at[pl.ds(n * wn, wn)], d_sem.at[n]) for n in range(nb)]
-    outs = [pltpu.make_async_copy(o_buf.at[:, pl.ds(c * wc, wc)], out_hbm.at[:, pl.ds(c * wc, wc)], o_sem.at[c]) for c in range(cb)]
     for copy in downs:
         copy.start()
     wx = 256
@@ -155,47 +145,39 @@
         tile = (rows // 16, 8, wc)
         even, odd = swap(low.reshape(tile), high.reshape(tile))
         both = jnp.concatenate([even[:, None], odd[:, None]], axis=1)
-        o_buf[:, at] = both.reshape(rows, wc).astype(BF)
-        outs[c].start()
-    for copy in outs:
-        copy.wait()
-
-
-def expert(x, w_gate, w_up, w_down, gate_scale, up_scale, down_scale, slots, nb=3, cb=4):
+        out_ref[:, at] = both.reshape(rows, wc).astype(BF)
+
+
+def expert(x, w_gate, w_up, w_down, gate_scale, up_scale, down_scale, slots, nb=1, cb=8):
     rows, half = x.shape
     width, ffw = w_gate.shape[1:]
     whole = pl.BlockSpec(memory_space=pltpu.VMEM)
     hbm = pl.BlockSpec(memory_space=pltpu.HBM)
     return pl.pallas_call(
         functools.partial(expert_body, slots=slots, nb=nb, cb=cb),
-        out_shape=pltpu.HBM((rows, half), BF),
+        out_shape=jax.ShapeDtypeStruct((rows, half), BF),
         in_specs=[whole, whole, whole, hbm, whole, whole, whole],
-        out_specs=hbm,
+        out_specs=whole,
         scratch_shapes=[
             pltpu.VMEM((ffw, width), BF),
             pltpu.VMEM((rows // 2, width), BF),
             pltpu.VMEM((rows // 2, ffw), BF),
-            pltpu.VMEM((rows, half), BF),
             pltpu.SemaphoreType.DMA((nb,)),
-            pltpu.SemaphoreType.DMA((cb,)),
         ],
-        compiler_params=pltpu.CompilerParams(vmem_limit_bytes=24 * MIB),
+        compiler_params=pltpu.CompilerParams(vmem_limit_bytes=20 * MIB),
         name="expert",
     )(x, w_gate, w_up, in_hbm(w_down), gate_scale, up_scale, down_scale)
 
 
-def mix_body(w_ref, r_hbm, out_hbm, r_buf, buf, in_sem, sem, *, steps):
-    count = w_ref.shape[0] // 4
-    half = r_buf.shape[1]
+def mix_body(ids_ref, weights_ref, r_ref, out_hbm, w_ref, buf, sem, *, experts, slots, steps):
+    count = ids_ref.shape[1]
+    w_ref[...] = table(ids_ref[...], weights_ref[...], experts, slots)
+    half = r_ref.shape[1]
     step = half // steps
     here = [pl.ds(n * step, step) for n in range(2 * steps)]
-    loads = [pltpu.make_async_copy(r_hbm.at[:, here[n]], r_buf.at[:, here[n]], in_sem.at[n]) for n in range(steps)]
     stores = [pltpu.make_async_copy(buf.at[:, here[n]], out_hbm.at[:, here[n]], sem.at[n]) for n in range(2 * steps)]
-    for copy in loads:
-        copy.start()
     for n in range(steps):
-        loads[n].wait()
-        both = dot(w_ref[...], r_buf[:, n * step : (n + 1) * step])
+        both = dot(w_ref[...], r_ref[:, n * step : (n + 1) * step])
         total = (both[: 2 * count] + both[2 * count :]).astype(BF)
         for h in range(2):
             at = h * half + n * step
@@ -205,24 +187,19 @@
         copy.wait()
 
 
-def mix(weights, results, steps=4):
-    count = weights.shape[0] // 4
+def mix(ids, weights, results, experts, slots, steps=4):
+    count = ids.shape[1]
     rows, half = results.shape
-    hbm = pl.BlockSpec(memory_space=pltpu.HBM)
+    whole = pl.BlockSpec(memory_space=pltpu.VMEM)
     return pl.pallas_call(
-        functools.partial(mix_body, steps=steps),
+        functools.partial(mix_body, experts=experts, slots=slots, steps=steps),
         out_shape=jax.ShapeDtypeStruct((count, 2 * half), BF),
-        in_specs=[pl.BlockSpec(memory_space=pltpu.VMEM), hbm],
-        out_specs=hbm,
-        scratch_shapes=[
-            pltpu.VMEM((rows, half), BF),
-            pltpu.VMEM((count, 2 * half), BF),
-            pltpu.SemaphoreType.DMA((steps,)),
-            pltpu.SemaphoreType.DMA((2 * steps,)),
-        ],
-        compiler_params=pltpu.CompilerParams(vmem_limit_bytes=16 * MIB),
+        in_specs=[whole, whole, whole],
+        out_specs=pl.BlockSpec(memory_space=pltpu.HBM),
+        scratch_shapes=[pltpu.VMEM((4 * count, rows), BF), pltpu.VMEM((count, 2 * half), BF), pltpu.SemaphoreType.DMA((2 * steps,))],
+        compiler_params=pltpu.CompilerParams(vmem_limit_bytes=8 * MIB),
         name="mix",
-    )(weights, results)
+    )(ids, weights, results)
 
 
 def exchange(x, experts):
@@ -239,7 +216,7 @@
     received = exchange(packed, experts)
     routed = expert(received, w_gate, w_up, w_down, gate_scale, up_scale, down_scale, slots)
     returned = exchange(routed, experts)
-    return mix(mixer(ids, weights, experts, slots), returned)
+    return mix(ids, weights, returned, experts, slots)
 
 
 def solution(mesh):

time: 140 us -> 135 us (0.964)
  blocking collectives: 62.8 us -> 119 us
  waiting for transfers between devices: 50.2 us -> 0 us
  starting transfers between devices: 5.83 us -> 0 us
  Pallas kernels: 20.7 us -> 15.4 us
    all_to_all x1 -> x2, blocking collectives: 62.8 us -> 119 us  [exchange(): lax.all_to_all(x, AXES, split_axis=0, concat_axis=0, tiled=True)]
    all_to_all x1 -> x0, waiting for transfers between devices: 50.2 us -> none  [exchange(): lax.all_to_all(x, AXES, split_axis=0, concat_axis=0, tiled=True)]
    all_to_all x1 -> x0, starting transfers between devices: 5.83 us -> none  [exchange(): lax.all_to_all(x, AXES, split_axis=0, concat_axis=0, tiled=True)]
    pallas_call x1, Pallas kernels: 13.5 us -> 10.1 us  [expert(): pl.pallas_call(functools.partial(expert_body, slots=slots, nb=nb, cb=cb),...]
    pallas_call x2 -> x1, Pallas kernels: 4.7 us -> 2.79 us  [mix(): pl.pallas_call(functools.partial(mix_body, experts=experts, slots=slots,...]
  transfers between devices with their start and end apart: 1 -> 0, of which waited for: 1 -> 0; matrix products, arithmetic and copies ran while one was open for 0% -> 0% of each run, Pallas kernels for 1% -> 0%
where the time goes in v3:
time: 135 us
  blocking collectives  119 us (88%)
  Pallas kernels  15.4 us (11%)
    all_to_all x2, blocking collectives, exchange(): lax.all_to_all(x, AXES, split_axis=0, concat_axis=0, tiled=True)  119 us
    pallas_call x1, Pallas kernels, expert(): pl.pallas_call(functools.partial(expert_body, slots=slots, nb=nb, cb=cb),...  10.1 us
    pallas_call x1, Pallas kernels, mix(): pl.pallas_call(functools.partial(mix_body, experts=experts, slots=slots,...  2.79 us

profile of v3, /device:TPU:1, one launch (start us, length us, event | category | flops | bytes accessed | tf_op | source)
XLA Modules:
  0.0 135.0 jit_solution(4848012853403399558)
XLA Ops:
  0.0 0.0 slice-start
  0.0 0.0 copy-start.2
  0.0 0.0 copy-start.4
  0.0 0.0 copy-start.5
  0.0 2.5 %pack.1 = bf16[1024,2048]{1,0:T(8,128)(2,1)S(1)} custom-call(s32[6,64]{1,0:T(8,128)} %bitcast.12, bf16[64,4096]{1,0:T(8,128)(2,1)} %tokens_hbm.1), custom_call_target="tpu_custom_call" | custom-call | tf_op jit(solution)/shard_map/pack/pallas_call | solution.py:71
  2.5 0.0 slice-start.1
  2.5 0.0 copy-start
  2.5 62.8 %all_to_all.10 = bf16[128,8,2048]{2,1,0:T(8,128)(2,1)S(1)} all-to-all(bf16[128,8,2048]{2,1,0:T(8,128)(2,1)S(1)} %bitcast.7), channel_id=1, replica_groups=mesh['node'=4,'wide'=32] {'node','wide'}, dimensions={0} | all-to-all | bytes 8388608 | tf_op jit(solution)/shard_map/all_to_all | solution.py:208
  65.3 0.0 slice-done
  65.3 0.0 copy-done.2
  65.3 0.0 copy-done.4
  65.4 0.0 copy-done.5
  65.4 0.0 slice-done.1
  65.4 0.0 copy-done
  65.4 10.1 %expert.1 = bf16[1024,2048]{1,0:T(8,128)(2,1)S(1)} custom-call(bf16[1024,2048]{1,0:T(8,128)(2,1)S(1)} %bitcast.8, bf16[1,4096,768]{2,1,0:T(8,128)(2,1)S(1)} %bitcast.11, bf16[1,4096,768]{2,1,0:T(8,128)(2,1)S(1)} %copy-done, bf16[1,768,4096]{2,1,0:T(8,128)(2,1)} %down_hbm.1, f32[1,768]{1,0:T(1,128)S(1)} %copy-done.4, f32[1,768]{1,0:T(1,128)S(1)} %copy-done.5, ...), custom_call_target="tpu_custom_call" | custom-call | tf_op jit(solution)/shard_map/expert/pallas_call | solution.py:156
  75.5 0.0 copy-start.1
  75.5 0.0 copy-start.3
  75.6 56.7 %all_to_all.11 = bf16[128,8,2048]{2,1,0:T(8,128)(2,1)S(1)} all-to-all(bf16[128,8,2048]{2,1,0:T(8,128)(2,1)S(1)} %bitcast.9), channel_id=1, replica_groups=mesh['node'=4,'wide'=32] {'node','wide'}, dimensions={0} | all-to-all | bytes 8388608 | tf_op jit(solution)/shard_map/all_to_all | solution.py:208
  132.2 0.0 copy-done.1
  132.2 0.0 copy-done.3
  132.2 2.8 %mix.1 = bf16[64,4096]{1,0:T(8,128)(2,1)} custom-call(s32[6,64]{1,0:T(8,128)S(1)} %bitcast.13, f32[6,64]{1,0:T(8,128)S(1)} %bitcast.14, bf16[1024,2048]{1,0:T(8,128)(2,1)S(1)} %bitcast.6), custom_call_target="tpu_custom_call" | custom-call | tf_op jit(solution)/shard_map/mix/pallas_call | solution.py:194
  (1 shorter events, 0.0 us)
Async XLA Ops:
  0.0 65.3 %slice-start = ((s8[6291456]{0:T(1024)(128)(4,1)}), s8[4194304]{0:T(1024)(128)(4,1)S(1)}, s32[]{:S(2)}) async-start(s8[6291456]{0:T(1024)(128)(4,1)} %bitcast.10), calls=%async_computation.2 | async-start | bytes 8388608
  0.0 65.3 %copy-start.2 = (f32[1,4096]{1,0:T(1,128)S(1)}, f32[1,4096]{1,0:T(1,128)}, u32[]{:S(2)}) copy-start(f32[1,4096]{1,0:T(1,128)} %down_s.1) | copy-start | bytes 49156
  0.0 65.3 %copy-start.4 = (f32[1,768]{1,0:T(1,128)S(1)}, f32[1,768]{1,0:T(1,128)}, u32[]{:S(2)}) copy-start(f32[1,768]{1,0:T(1,128)} %gate_s.1) | copy-start | bytes 9220
  0.0 65.3 %copy-start.5 = (f32[1,768]{1,0:T(1,128)S(1)}, f32[1,768]{1,0:T(1,128)}, u32[]{:S(2)}) copy-start(f32[1,768]{1,0:T(1,128)} %up_s.1) | copy-start | bytes 9220
  2.5 62.9 %slice-start.1 = ((s8[6291456]{0:T(1024)(128)(4,1)}), s8[2097152]{0:T(1024)(128)(4,1)S(1)}, s32[]{:S(2)}) async-start(s8[6291456]{0:T(1024)(128)(4,1)} %bitcast.10), calls=%async_computation.3 | async-start | bytes 4194304
  2.5 62.8 %copy-start = (bf16[1,4096,768]{2,1,0:T(8,128)(2,1)S(1)}, bf16[1,4096,768]{2,1,0:T(8,128)(2,1)}, u32[]{:S(2)}) copy-start(bf16[1,4096,768]{2,1,0:T(8,128)(2,1)} %up_ref.1) | copy-start | bytes 18874372
  75.5 56.7 %copy-start.1 = (s32[64,6]{0,1:T(8,128)S(1)}, s32[64,6]{0,1:T(8,128)}, u32[]{:S(2)}) copy-start(s32[64,6]{0,1:T(8,128)} %param.10) | copy-start | bytes 4612
  75.5 56.7 %copy-start.3 = (f32[64,6]{0,1:T(8,128)S(1)}, f32[64,6]{0,1:T(8,128)}, u32[]{:S(2)}) copy-start(f32[64,6]{0,1:T(8,128)} %param.11) | copy-start | bytes 4612

commit v4 on v3

--- a/solution.py
+++ b/solution.py
@@ -55,14 +55,14 @@
     slot = (iota(shape, 0) % slots).astype(F32)
     half_of = iota(shape, 0) // slots % 2 == iota(shape, 1) // count
     ids_copy.wait()
-    wide = dot(spread, codes(ids_ref[...], experts))
-    hot = onehot((wide == slot) & half_of)
+    code = codes(ids_ref[...], experts)
+    step = rows // 2
+    wide = [dot(spread[n * step : (n + 1) * step], code) for n in range(2)]
+    hot = [onehot((wide[n] == slot[n * step : (n + 1) * step]) & half_of[n * step : (n + 1) * step]) for n in range(2)]
     tok_copy.wait()
-    step = half // steps
-    for n in range(steps):
-        at = slice(n * step, (n + 1) * step)
-        stacked = jnp.concatenate([tok_ref[:, at], tok_ref[:, half + n * step : half + (n + 1) * step]], axis=0)
-        out_ref[:, at] = dot(hot, stacked).astype(BF)
+    stacked = jnp.concatenate([tok_ref[:, :half], tok_ref[:, half:]], axis=0)
+    for n in range(2):
+        out_ref[n * step : (n + 1) * step, :] = dot(hot[n], stacked).astype(BF)
 
 
 def pack(ids, tokens, experts, slots, steps=4):
@@ -83,27 +83,29 @@
     )(in_hbm(ids), in_hbm(tokens))
 
 
-def table(ids, weights, experts, slots):
+def table(ids, weights, out_ref, experts, slots):
     top, count = ids.shape
     rows = experts * 2 * slots
     code = codes(ids, experts)
     chosen = jnp.zeros((experts, count), F32)
     for k in range(top):
         chosen = chosen + jnp.where(iota((experts, count), 0) == ids[k : k + 1, :], weights[k : k + 1, :], 0.0)
+    high = chosen.astype(BF)
+    low = (chosen - high.astype(F32)).astype(BF)
+    yield
     twice = onehot(iota((count, 2 * count), 0) == iota((count, 2 * count), 1) % count)
+    parts = [dot(part, twice).astype(BF) for part in (high, low)]
     spread = onehot(iota((experts, rows), 1) // (2 * slots) == iota((experts, rows), 0))
     shape = (2 * count, rows)
+    yield
     wide = dot(code, spread, ((0,), (0,)))
     slot = (iota(shape, 1) % slots).astype(F32)
     here = (wide == slot) & (iota(shape, 1) // slots % 2 == iota(shape, 0) // count)
-    high = chosen.astype(BF)
-    low = (chosen - high.astype(F32)).astype(BF)
-    parts = []
-    for part in (high, low):
-        part = dot(part, twice).astype(BF)
+    for n, part in enumerate(parts):
+        yield
         part = dot(part, spread, ((0,), (0,)))
-        parts.append(jnp.where(here, part, 0.0).astype(BF))
-    return jnp.concatenate(parts, axis=0)
+        out_ref[n * 2 * count : (n + 1) * 2 * count, :] = jnp.where(here, part, 0.0).astype(BF)
+    yield
 
 
 def swap(first, second):
@@ -115,7 +117,7 @@
 
 
 def expert_body(
-    x_ref, gate_ref, up_ref, down_hbm, gate_s, up_s, down_s, out_ref, d_buf, xs, hid, d_sem, *, slots, nb, cb
+    x_ref, gate_ref, up_ref, down_hbm, gate_s, up_s, down_s, ids_ref, weights_ref, out_ref, table_ref, d_buf, xs, hid, d_sem, *, slots, nb, cb
 ):
     rows, half = x_ref.shape
     ffw = gate_s.shape[1]
@@ -124,6 +126,7 @@
     downs = [pltpu.make_async_copy(down_hbm.at[0, pl.ds(n * wn, wn)], d_buf.at[pl.ds(n * wn, wn)], d_sem.at[n]) for n in range(nb)]
     for copy in downs:
         copy.start()
+    steps = table(ids_ref[...], weights_ref[...], table_ref, rows // (2 * slots), slots)
     wx = 256
     for n in range(half // wx):
         at = slice(n * wx, (n + 1) * wx)
@@ -139,6 +142,7 @@
     for copy in downs:
         copy.wait()
     for c in range(cb):
+        next(steps, None)
         at, to = slice(c * wc, (c + 1) * wc), slice(half + c * wc, half + (c + 1) * wc)
         low = dot(hid[...], d_buf[:, at]) * down_s[:, at]
         high = dot(hid[...], d_buf[:, to]) * down_s[:, to]
@@ -148,16 +152,16 @@
         out_ref[:, at] = both.reshape(rows, wc).astype(BF)
 
 
-def expert(x, w_gate, w_up, w_down, gate_scale, up_scale, down_scale, slots, nb=1, cb=8):
+def expert(x, w_gate, w_up, w_down, gate_scale, up_scale, down_scale, ids, weights, slots, nb=1, cb=8):
     rows, half = x.shape
     width, ffw = w_gate.shape[1:]
     whole = pl.BlockSpec(memory_space=pltpu.VMEM)
     hbm = pl.BlockSpec(memory_space=pltpu.HBM)
     return pl.pallas_call(
         functools.partial(expert_body, slots=slots, nb=nb, cb=cb),
-        out_shape=jax.ShapeDtypeStruct((rows, half), BF),
-        in_specs=[whole, whole, whole, hbm, whole, whole, whole],
-        out_specs=whole,
+        out_shape=[jax.ShapeDtypeStruct((rows, half), BF), jax.ShapeDtypeStruct((4 * ids.shape[1], rows), BF)],
+        in_specs=[whole, whole, whole, hbm] + [whole] * 5,
+        out_specs=[whole, whole],
         scratch_shapes=[
             pltpu.VMEM((ffw, width), BF),
             pltpu.VMEM((rows // 2, width), BF),
@@ -166,12 +170,11 @@
         ],
         compiler_params=pltpu.CompilerParams(vmem_limit_bytes=20 * MIB),
         name="expert",
-    )(x, w_gate, w_up, in_hbm(w_down), gate_scale, up_scale, down_scale)
-
-
-def mix_body(ids_ref, weights_ref, r_ref, out_hbm, w_ref, buf, sem, *, experts, slots, steps):
-    count = ids_ref.shape[1]
-    w_ref[...] = table(ids_ref[...], weights_ref[...], experts, slots)
+    )(x, w_gate, w_up, in_hbm(w_down), gate_scale, up_scale, down_scale, ids, weights)
+
+
+def mix_body(w_ref, r_ref, out_hbm, buf, sem, *, steps):
+    count = w_ref.shape[0] // 4
     half = r_ref.shape[1]
     step = half // steps
     here = [pl.ds(n * step, step) for n in range(2 * steps)]
@@ -187,19 +190,19 @@
         copy.wait()
 
 
-def mix(ids, weights, results, experts, slots, steps=4):
-    count = ids.shape[1]
+def mix(weights, results, steps=4):
+    count = weights.shape[0] // 4
     rows, half = results.shape
     whole = pl.BlockSpec(memory_space=pltpu.VMEM)
     return pl.pallas_call(
-        functools.partial(mix_body, experts=experts, slots=slots, steps=steps),
+        functools.partial(mix_body, steps=steps),
         out_shape=jax.ShapeDtypeStruct((count, 2 * half), BF),
-        in_specs=[whole, whole, whole],
+        in_specs=[whole, whole],
         out_specs=pl.BlockSpec(memory_space=pltpu.HBM),
-        scratch_shapes=[pltpu.VMEM((4 * count, rows), BF), pltpu.VMEM((count, 2 * half), BF), pltpu.SemaphoreType.DMA((2 * steps,))],
+        scratch_shapes=[pltpu.VMEM((count, 2 * half), BF), pltpu.SemaphoreType.DMA((2 * steps,))],
         compiler_params=pltpu.CompilerParams(vmem_limit_bytes=8 * MIB),
         name="mix",
-    )(ids, weights, results)
+    )(weights, results)
 
 
 def exchange(x, experts):
@@ -214,9 +217,10 @@
     ids, weights = expert_ids.T, gate_weights.T
     packed = pack(ids, tokens, experts, slots)
     received = exchange(packed, experts)
-    routed = expert(received, w_gate, w_up, w_down, gate_scale, up_scale, down_scale, slots)
+    scales = (gate_scale, up_scale, down_scale)
+    routed, chosen = expert(received, w_gate, w_up, w_down, *scales, ids, weights, slots)
     returned = exchange(routed, experts)
-    return mix(ids, weights, returned, experts, slots)
+    return mix(chosen, returned)
 
 
 def solution(mesh):

time: 135 us -> 135 us (level)
  no operation moved by 1% of the time
where the time goes in v4:
time: 135 us
  blocking collectives  119 us (88%)
  Pallas kernels  15 us (11%)
    all_to_all x2, blocking collectives, exchange(): lax.all_to_all(x, AXES, split_axis=0, concat_axis=0, tiled=True)  119 us
    pallas_call x1, Pallas kernels, expert(): pl.pallas_call(functools.partial(expert_body, slots=slots, nb=nb, cb=cb),...  10.6 us

profile of v4, /device:TPU:1, one launch (start us, length us, event | category | flops | bytes accessed | tf_op | source)
XLA Modules:
  0.0 134.6 jit_solution(560421964498972590)
XLA Ops:
  0.0 0.0 slice-start
  0.0 0.0 copy-start.1
  0.0 0.0 copy-start.2
  0.0 0.0 copy-start.3
  0.0 0.0 copy-start.5
  0.0 2.5 %pack.1 = bf16[1024,2048]{1,0:T(8,128)(2,1)S(1)} custom-call(s32[6,64]{1,0:T(8,128)} %bitcast.12, bf16[64,4096]{1,0:T(8,128)(2,1)} %tokens_hbm.1), custom_call_target="tpu_custom_call" | custom-call | tf_op jit(solution)/shard_map/pack/pallas_call | solution.py:71
  2.5 0.0 slice-start.1
  2.5 0.0 copy-start
  2.5 0.0 copy-start.4
  2.6 62.8 %all_to_all.10 = bf16[128,8,2048]{2,1,0:T(8,128)(2,1)S(1)} all-to-all(bf16[128,8,2048]{2,1,0:T(8,128)(2,1)S(1)} %bitcast.7), channel_id=1, replica_groups=mesh['node'=4,'wide'=32] {'node','wide'}, dimensions={0} | all-to-all | bytes 8388608 | tf_op jit(solution)/shard_map/all_to_all | solution.py:211
  65.4 0.0 slice-done
  65.4 0.0 copy-done.1
  65.4 0.0 copy-done.2
  65.4 0.0 copy-done.3
  65.4 0.0 copy-done.5
  65.4 0.0 slice-done.1
  65.4 0.0 copy-done
  65.4 0.0 copy-done.4
  65.4 10.6 %expert.1 = (bf16[1024,2048]{1,0:T(8,128)(2,1)S(1)}, bf16[256,1024]{1,0:T(8,128)(2,1)S(1)}) custom-call(bf16[1024,2048]{1,0:T(8,128)(2,1)S(1)} %bitcast.8, bf16[1,4096,768]{2,1,0:T(8,128)(2,1)S(1)} %bitcast.10, bf16[1,4096,768]{2,1,0:T(8,128)(2,1)S(1)} %copy-done, bf16[1,768,4096]{2,1,0:T(8,128)(2,1)} %down_hbm.1, f32[1,768]{1,0:T(1,128)S(1)} %copy-done.4, ...), custom_call_target="tpu_custom_call" | custom-call | tf_op jit(solution)/shard_map/expert/pallas_call | solution.py:160
  76.0 56.7 %all_to_all.11 = bf16[128,8,2048]{2,1,0:T(8,128)(2,1)S(1)} all-to-all(bf16[128,8,2048]{2,1,0:T(8,128)(2,1)S(1)} %bitcast.11), channel_id=1, replica_groups=mesh['node'=4,'wide'=32] {'node','wide'}, dimensions={0} | all-to-all | bytes 8388608 | tf_op jit(solution)/shard_map/all_to_all | solution.py:211
  132.7 2.0 %mix.1 = bf16[64,4096]{1,0:T(8,128)(2,1)} custom-call(bf16[256,1024]{1,0:T(8,128)(2,1)S(1)} %get-tuple-element.7.w_ref, bf16[1024,2048]{1,0:T(8,128)(2,1)S(1)} %bitcast.6), custom_call_target="tpu_custom_call" | custom-call | tf_op jit(solution)/shard_map/mix/pallas_call | solution.py:197
  (1 shorter events, 0.0 us)
Async XLA Ops:
  0.0 65.4 %slice-start = ((s8[6291456]{0:T(1024)(128)(4,1)}), s8[4194304]{0:T(1024)(128)(4,1)S(1)}, s32[]{:S(2)}) async-start(s8[6291456]{0:T(1024)(128)(4,1)} %bitcast.9), calls=%async_computation.2 | async-start | bytes 8388608
  0.0 65.4 %copy-start.1 = (f32[1,4096]{1,0:T(1,128)S(1)}, f32[1,4096]{1,0:T(1,128)}, u32[]{:S(2)}) copy-start(f32[1,4096]{1,0:T(1,128)} %down_s.1) | copy-start | bytes 49156
  0.0 65.4 %copy-start.2 = (s32[64,6]{0,1:T(8,128)S(1)}, s32[64,6]{0,1:T(8,128)}, u32[]{:S(2)}) copy-start(s32[64,6]{0,1:T(8,128)} %param.10) | copy-start | bytes 4612
  0.0 65.4 %copy-start.3 = (f32[64,6]{0,1:T(8,128)S(1)}, f32[64,6]{0,1:T(8,128)}, u32[]{:S(2)}) copy-start(f32[64,6]{0,1:T(8,128)} %param.11) | copy-start | bytes 4612
  0.0 65.4 %copy-start.5 = (f32[1,768]{1,0:T(1,128)S(1)}, f32[1,768]{1,0:T(1,128)}, u32[]{:S(2)}) copy-start(f32[1,768]{1,0:T(1,128)} %up_s.1) | copy-start | bytes 9220
  2.5 62.9 %slice-start.1 = ((s8[6291456]{0:T(1024)(128)(4,1)}), s8[2097152]{0:T(1024)(128)(4,1)S(1)}, s32[]{:S(2)}) async-start(s8[6291456]{0:T(1024)(128)(4,1)} %bitcast.9), calls=%async_computation.3 | async-start | bytes 4194304
  2.5 62.9 %copy-start = (bf16[1,4096,768]{2,1,0:T(8,128)(2,1)S(1)}, bf16[1,4096,768]{2,1,0:T(8,128)(2,1)}, u32[]{:S(2)}) copy-start(bf16[1,4096,768]{2,1,0:T(8,128)(2,1)} %up_ref.1) | copy-start | bytes 18874372
  2.5 62.9 %copy-start.4 = (f32[1,768]{1,0:T(1,128)S(1)}, f32[1,768]{1,0:T(1,128)}, u32[]{:S(2)}) copy-start(f32[1,768]{1,0:T(1,128)} %gate_s.1) | copy-start | bytes 9220

commit v5 on v4

--- a/solution.py
+++ b/solution.py
@@ -86,25 +86,28 @@
 def table(ids, weights, out_ref, experts, slots):
     top, count = ids.shape
     rows = experts * 2 * slots
-    code = codes(ids, experts)
+    shape = (count, rows)
+    named = jnp.zeros((experts, count), F32)
     chosen = jnp.zeros((experts, count), F32)
     for k in range(top):
-        chosen = chosen + jnp.where(iota((experts, count), 0) == ids[k : k + 1, :], weights[k : k + 1, :], 0.0)
+        here = iota((experts, count), 0) == ids[k : k + 1, :]
+        named = jnp.where(here, 1.0, named)
+        chosen = jnp.where(here, weights[k : k + 1, :], chosen)
+    before = onehot(iota((count, count), 0) < iota((count, count), 1))
+    code = (dot(named.astype(BF), before) + 8.0 * (1.0 - named)).astype(BF)
     high = chosen.astype(BF)
     low = (chosen - high.astype(F32)).astype(BF)
-    yield
-    twice = onehot(iota((count, 2 * count), 0) == iota((count, 2 * count), 1) % count)
-    parts = [dot(part, twice).astype(BF) for part in (high, low)]
     spread = onehot(iota((experts, rows), 1) // (2 * slots) == iota((experts, rows), 0))
-    shape = (2 * count, rows)
     yield
     wide = dot(code, spread, ((0,), (0,)))
-    slot = (iota(shape, 1) % slots).astype(F32)
-    here = (wide == slot) & (iota(shape, 1) // slots % 2 == iota(shape, 0) // count)
-    for n, part in enumerate(parts):
+    here = wide == (iota(shape, 1) % slots).astype(F32)
+    second = iota(shape, 1) // slots % 2 == 1
+    for n, part in enumerate((high, low)):
         yield
-        part = dot(part, spread, ((0,), (0,)))
-        out_ref[n * 2 * count : (n + 1) * 2 * count, :] = jnp.where(here, part, 0.0).astype(BF)
+        part = jnp.where(here, dot(part, spread, ((0,), (0,))), 0.0)
+        at = 2 * n * count
+        out_ref[at : at + count, :] = jnp.where(second, 0.0, part).astype(BF)
+        out_ref[at + count : at + 2 * count, :] = jnp.where(second, part, 0.0).astype(BF)
     yield
 
 

time: 135 us -> 135 us (level)
  no operation moved by 1% of the time
where the time goes in v5:
time: 135 us; the launch traced here: 134 us
  blocking collectives  119 us (88%)
  Pallas kernels  14.9 us (11%)
    all_to_all x2, blocking collectives, exchange(): lax.all_to_all(x, AXES, split_axis=0, concat_axis=0, tiled=True)  119 us
    pallas_call x1, Pallas kernels, expert(): pl.pallas_call(functools.partial(expert_body, slots=slots, nb=nb, cb=cb),...  10.4 us

profile of v5, /device:TPU:1, one launch (start us, length us, event | category | flops | bytes accessed | tf_op | source)
XLA Modules:
  0.0 134.5 jit_solution(6077402819309282932)
XLA Ops:
  0.0 0.0 slice-start
  0.0 0.0 copy-start.1
  0.0 0.0 copy-start.2
  0.0 0.0 copy-start.3
  0.0 0.0 copy-start.5
  0.0 2.5 %pack.1 = bf16[1024,2048]{1,0:T(8,128)(2,1)S(1)} custom-call(s32[6,64]{1,0:T(8,128)} %bitcast.12, bf16[64,4096]{1,0:T(8,128)(2,1)} %tokens_hbm.1), custom_call_target="tpu_custom_call" | custom-call | tf_op jit(solution)/shard_map/pack/pallas_call | solution.py:71
  2.5 0.0 slice-start.1
  2.5 0.0 copy-start
  2.5 0.0 copy-start.4
  2.6 62.8 %all_to_all.10 = bf16[128,8,2048]{2,1,0:T(8,128)(2,1)S(1)} all-to-all(bf16[128,8,2048]{2,1,0:T(8,128)(2,1)S(1)} %bitcast.7), channel_id=1, replica_groups=mesh['node'=4,'wide'=32] {'node','wide'}, dimensions={0} | all-to-all | bytes 8388608 | tf_op jit(solution)/shard_map/all_to_all | solution.py:214
  65.4 0.0 slice-done
  65.4 0.0 copy-done.1
  65.4 0.0 copy-done.2
  65.4 0.0 copy-done.3
  65.4 0.0 copy-done.5
  65.4 0.0 slice-done.1
  65.4 0.0 copy-done
  65.4 0.0 copy-done.4
  65.4 10.4 %expert.1 = (bf16[1024,2048]{1,0:T(8,128)(2,1)S(1)}, bf16[256,1024]{1,0:T(8,128)(2,1)S(1)}) custom-call(bf16[1024,2048]{1,0:T(8,128)(2,1)S(1)} %bitcast.8, bf16[1,4096,768]{2,1,0:T(8,128)(2,1)S(1)} %bitcast.10, bf16[1,4096,768]{2,1,0:T(8,128)(2,1)S(1)} %copy-done, bf16[1,768,4096]{2,1,0:T(8,128)(2,1)} %down_hbm.1, f32[1,768]{1,0:T(1,128)S(1)} %copy-done.4, ...), custom_call_target="tpu_custom_call" | custom-call | tf_op jit(solution)/shard_map/expert/pallas_call | solution.py:163
  75.9 56.7 %all_to_all.11 = bf16[128,8,2048]{2,1,0:T(8,128)(2,1)S(1)} all-to-all(bf16[128,8,2048]{2,1,0:T(8,128)(2,1)S(1)} %bitcast.11), channel_id=1, replica_groups=mesh['node'=4,'wide'=32] {'node','wide'}, dimensions={0} | all-to-all | bytes 8388608 | tf_op jit(solution)/shard_map/all_to_all | solution.py:214
  132.5 2.0 %mix.1 = bf16[64,4096]{1,0:T(8,128)(2,1)} custom-call(bf16[256,1024]{1,0:T(8,128)(2,1)S(1)} %get-tuple-element.7.w_ref, bf16[1024,2048]{1,0:T(8,128)(2,1)S(1)} %bitcast.6), custom_call_target="tpu_custom_call" | custom-call | tf_op jit(solution)/shard_map/mix/pallas_call | solution.py:200
  (1 shorter events, 0.0 us)
Async XLA Ops:
  0.0 65.4 %slice-start = ((s8[6291456]{0:T(1024)(128)(4,1)}), s8[4194304]{0:T(1024)(128)(4,1)S(1)}, s32[]{:S(2)}) async-start(s8[6291456]{0:T(1024)(128)(4,1)} %bitcast.9), calls=%async_computation.2 | async-start | bytes 8388608
  0.0 65.4 %copy-start.1 = (f32[1,4096]{1,0:T(1,128)S(1)}, f32[1,4096]{1,0:T(1,128)}, u32[]{:S(2)}) copy-start(f32[1,4096]{1,0:T(1,128)} %down_s.1) | copy-start | bytes 49156
  0.0 65.4 %copy-start.2 = (s32[64,6]{0,1:T(8,128)S(1)}, s32[64,6]{0,1:T(8,128)}, u32[]{:S(2)}) copy-start(s32[64,6]{0,1:T(8,128)} %param.10) | copy-start | bytes 4612
  0.0 65.4 %copy-start.3 = (f32[64,6]{0,1:T(8,128)S(1)}, f32[64,6]{0,1:T(8,128)}, u32[]{:S(2)}) copy-start(f32[64,6]{0,1:T(8,128)} %param.11) | copy-start | bytes 4612
  0.0 65.4 %copy-start.5 = (f32[1,768]{1,0:T(1,128)S(1)}, f32[1,768]{1,0:T(1,128)}, u32[]{:S(2)}) copy-start(f32[1,768]{1,0:T(1,128)} %up_s.1) | copy-start | bytes 9220
  2.5 62.9 %slice-start.1 = ((s8[6291456]{0:T(1024)(128)(4,1)}), s8[2097152]{0:T(1024)(128)(4,1)S(1)}, s32[]{:S(2)}) async-start(s8[6291456]{0:T(1024)(128)(4,1)} %bitcast.9), calls=%async_computation.3 | async-start | bytes 4194304
  2.5 62.9 %copy-start = (bf16[1,4096,768]{2,1,0:T(8,128)(2,1)S(1)}, bf16[1,4096,768]{2,1,0:T(8,128)(2,1)}, u32[]{:S(2)}) copy-start(bf16[1,4096,768]{2,1,0:T(8,128)(2,1)} %up_ref.1) | copy-start | bytes 18874372
  2.5 62.9 %copy-start.4 = (f32[1,768]{1,0:T(1,128)S(1)}, f32[1,768]{1,0:T(1,128)}, u32[]{:S(2)}) copy-start(f32[1,768]{1,0:T(1,128)} %gate_s.1) | copy-start | bytes 9220

commit v6 on v5

--- a/solution.py
+++ b/solution.py
@@ -131,17 +131,21 @@
         copy.start()
     steps = table(ids_ref[...], weights_ref[...], table_ref, rows // (2 * slots), slots)
     wx = 256
-    for n in range(half // wx):
-        at = slice(n * wx, (n + 1) * wx)
-        pairs = x_ref[:, at].astype(F32).reshape(rows // 16, 2, 8, wx)
-        low, high = swap(pairs[:, 0], pairs[:, 1])
-        xs[:, at] = low.reshape(rows // 2, wx).astype(BF)
-        xs[:, half + n * wx : half + (n + 1) * wx] = high.reshape(rows // 2, wx).astype(BF)
-    for n in range(nb):
-        at = slice(n * wn, (n + 1) * wn)
-        gate = dot(xs[...], gate_ref[0, :, at]) * gate_s[:, at]
-        up = dot(xs[...], up_ref[0, :, at]) * up_s[:, at]
-        hid[:, at] = (gate / (1.0 + jnp.exp(-gate)) * up).astype(BF)
+    gate = None
+    for g in range(2):
+        for n in range(g * half // wx // 2, (g + 1) * half // wx // 2):
+            at = slice(n * wx, (n + 1) * wx)
+            pairs = x_ref[:, at].astype(F32).reshape(rows // 16, 2, 8, wx)
+            low, high = swap(pairs[:, 0], pairs[:, 1])
+            xs[:, at] = low.reshape(rows // 2, wx).astype(BF)
+            xs[:, half + n * wx : half + (n + 1) * wx] = high.reshape(rows // 2, wx).astype(BF)
+        for h in range(2):
+            at = slice(h * half + g * half // 2, h * half + (g + 1) * half // 2)
+            part = dot(xs[:, at], gate_ref[0, at, :])
+            gate = part if gate is None else gate + part
+    gate = gate * gate_s[...]
+    up = dot(xs[...], up_ref[0]) * up_s[...]
+    hid[...] = (gate / (1.0 + jnp.exp(-gate)) * up).astype(BF)
     for copy in downs:
         copy.wait()
     for c in range(cb):

time: 135 us -> 135 us (level)
  no operation moved by 1% of the time
where the time goes in v6:
time: 135 us
  blocking collectives  119 us (88%)
  Pallas kernels  14.9 us (11%)
    all_to_all x2, blocking collectives, exchange(): lax.all_to_all(x, AXES, split_axis=0, concat_axis=0, tiled=True)  119 us
    pallas_call x1, Pallas kernels, expert(): pl.pallas_call(functools.partial(expert_body, slots=slots, nb=nb, cb=cb),...  10.5 us

profile of v6, /device:TPU:1, one launch (start us, length us, event | category | flops | bytes accessed | tf_op | source)
XLA Modules:
  0.0 134.5 jit_solution(6772142561627167530)
XLA Ops:
  0.0 0.0 slice-start
  0.0 0.0 copy-start.1
  0.0 0.0 copy-start.2
  0.0 0.0 copy-start.3
  0.0 0.0 copy-start.5
  0.0 2.5 %pack.1 = bf16[1024,2048]{1,0:T(8,128)(2,1)S(1)} custom-call(s32[6,64]{1,0:T(8,128)} %bitcast.12, bf16[64,4096]{1,0:T(8,128)(2,1)} %tokens_hbm.1), custom_call_target="tpu_custom_call" | custom-call | tf_op jit(solution)/shard_map/pack/pallas_call | solution.py:71
  2.5 0.0 slice-start.1
  2.5 0.0 copy-start
  2.5 0.0 copy-start.4
  2.6 62.8 %all_to_all.10 = bf16[128,8,2048]{2,1,0:T(8,128)(2,1)S(1)} all-to-all(bf16[128,8,2048]{2,1,0:T(8,128)(2,1)S(1)} %bitcast.7), channel_id=1, replica_groups=mesh['node'=4,'wide'=32] {'node','wide'}, dimensions={0} | all-to-all | bytes 8388608 | tf_op jit(solution)/shard_map/all_to_all | solution.py:218
  65.4 0.0 slice-done
  65.4 0.0 copy-done.1
  65.4 0.0 copy-done.2
  65.4 0.0 copy-done.3
  65.4 0.0 copy-done.5
  65.4 0.0 slice-done.1
  65.4 0.0 copy-done
  65.4 0.0 copy-done.4
  65.4 10.5 %expert.1 = (bf16[1024,2048]{1,0:T(8,128)(2,1)S(1)}, bf16[256,1024]{1,0:T(8,128)(2,1)S(1)}) custom-call(bf16[1024,2048]{1,0:T(8,128)(2,1)S(1)} %bitcast.8, bf16[1,4096,768]{2,1,0:T(8,128)(2,1)S(1)} %bitcast.10, bf16[1,4096,768]{2,1,0:T(8,128)(2,1)S(1)} %copy-done, bf16[1,768,4096]{2,1,0:T(8,128)(2,1)} %down_hbm.1, f32[1,768]{1,0:T(1,128)S(1)} %copy-done.4, ...), custom_call_target="tpu_custom_call" | custom-call | tf_op jit(solution)/shard_map/expert/pallas_call | solution.py:167
  75.9 56.7 %all_to_all.11 = bf16[128,8,2048]{2,1,0:T(8,128)(2,1)S(1)} all-to-all(bf16[128,8,2048]{2,1,0:T(8,128)(2,1)S(1)} %bitcast.11), channel_id=1, replica_groups=mesh['node'=4,'wide'=32] {'node','wide'}, dimensions={0} | all-to-all | bytes 8388608 | tf_op jit(solution)/shard_map/all_to_all | solution.py:218
  132.6 2.0 %mix.1 = bf16[64,4096]{1,0:T(8,128)(2,1)} custom-call(bf16[256,1024]{1,0:T(8,128)(2,1)S(1)} %get-tuple-element.7.w_ref, bf16[1024,2048]{1,0:T(8,128)(2,1)S(1)} %bitcast.6), custom_call_target="tpu_custom_call" | custom-call | tf_op jit(solution)/shard_map/mix/pallas_call | solution.py:204
  (1 shorter events, 0.0 us)
Async XLA Ops:
  0.0 65.4 %slice-start = ((s8[6291456]{0:T(1024)(128)(4,1)}), s8[4194304]{0:T(1024)(128)(4,1)S(1)}, s32[]{:S(2)}) async-start(s8[6291456]{0:T(1024)(128)(4,1)} %bitcast.9), calls=%async_computation.2 | async-start | bytes 8388608
  0.0 65.4 %copy-start.1 = (f32[1,4096]{1,0:T(1,128)S(1)}, f32[1,4096]{1,0:T(1,128)}, u32[]{:S(2)}) copy-start(f32[1,4096]{1,0:T(1,128)} %down_s.1) | copy-start | bytes 49156
  0.0 65.4 %copy-start.2 = (s32[64,6]{0,1:T(8,128)S(1)}, s32[64,6]{0,1:T(8,128)}, u32[]{:S(2)}) copy-start(s32[64,6]{0,1:T(8,128)} %param.10) | copy-start | bytes 4612
  0.0 65.4 %copy-start.3 = (f32[64,6]{0,1:T(8,128)S(1)}, f32[64,6]{0,1:T(8,128)}, u32[]{:S(2)}) copy-start(f32[64,6]{0,1:T(8,128)} %param.11) | copy-start | bytes 4612
  0.0 65.4 %copy-start.5 = (f32[1,768]{1,0:T(1,128)S(1)}, f32[1,768]{1,0:T(1,128)}, u32[]{:S(2)}) copy-start(f32[1,768]{1,0:T(1,128)} %up_s.1) | copy-start | bytes 9220
  2.5 62.9 %slice-start.1 = ((s8[6291456]{0:T(1024)(128)(4,1)}), s8[2097152]{0:T(1024)(128)(4,1)S(1)}, s32[]{:S(2)}) async-start(s8[6291456]{0:T(1024)(128)(4,1)} %bitcast.9), calls=%async_computation.3 | async-start | bytes 4194304
  2.5 62.9 %copy-start = (bf16[1,4096,768]{2,1,0:T(8,128)(2,1)S(1)}, bf16[1,4096,768]{2,1,0:T(8,128)(2,1)}, u32[]{:S(2)}) copy-start(bf16[1,4096,768]{2,1,0:T(8,128)(2,1)} %up_ref.1) | copy-start | bytes 18874372
  2.5 62.9 %copy-start.4 = (f32[1,768]{1,0:T(1,128)S(1)}, f32[1,768]{1,0:T(1,128)}, u32[]{:S(2)}) copy-start(f32[1,768]{1,0:T(1,128)} %gate_s.1) | copy-start | bytes 9220
